TPU v7x, 256 devices: a whole 4x4x8 slice. The times are simulated.
256 devices in a mesh: tm: 16 (over z_hi, y), space: 16 (over z_lo, x, core).
Axes of the slice: x: 4, y: 4, z: 8 (z_hi: 4, z_lo: 2; z = z_hi * 2 + z_lo), core: 2. Of those that a mesh axis runs over, the one named last changes fastest.
Arguments:
- amplitude: float32 [160, 384, 512], P('tm', 'space'), may hold values from 0.3 to 3
- phase: float32 [160, 384, 512], P('tm', 'space'), may hold values from -3.140625 to 3.140625
- validity: int32 [384, 512], P('space'), may hold values 0 or 1
- iterations: int32 [16], P('tm'), may hold values from 10 to 20, as said below
- reference_date: int32 [16], P('tm'), may hold values from 0 to 9
Outputs:
- linked: float32 [2, 160, 384, 512], P(None, 'tm', 'space')
Inputs may be any that keep to these rules, and one draw needn't show every extreme that they name: Every ministack takes between 10 and 20 iterations, and some ministack takes exactly 20.
All inputs are finite; a program needn't handle non-finite values. No bound on the sum of `validity` on one device may be relied on, other than what follows from the above.
Results may differ from a plain program's by a relative error of at most 0.0003.
Values sent between devices are 32-bit elements; how exact they have to be, the bound alone decides.
A program may use at most 64 MiB of HBM per device.

v0:
```python
import math

import jax
import jax.numpy as jnp
from jax import lax
from jax.sharding import PartitionSpec as P

WIN_ROWS = 11
WIN_COLS = 5
ITERS = 20


masked_weight = 0.125
link_floor = 0.03


def extended_2(value, sides, width):
    for axis, dim in sides:
        count, length = (lax.axis_size(axis), value.shape[dim])
        up = [(i, (i + 1) % count) for i in range(count - 1)]
        down = [(j, i) for i, j in up]
        last = lax.slice_in_dim(value, length - width, length, axis=dim)
        leading = lax.slice_in_dim(value, 0, width, axis=dim)
        before = lax.ppermute(last, axis, up)
        after = lax.ppermute(leading, axis, down)
        value = jnp.concatenate([before, value, after], axis=dim)
    return value


def shifted(block, axis, distance):
    devices = range(lax.axis_size(axis))
    route = [(i - distance, i) for i in devices if i - distance in devices]
    return lax.ppermute(block, axis, route)


def prefix(value, axis, combine, identity):
    count, mine = (lax.axis_size(axis), lax.axis_index(axis))
    everything = jax.tree.map(lambda part: lax.all_gather(part, axis), value)
    start = jax.tree.map(
        lambda part, zero: jnp.broadcast_to(jnp.asarray(zero, part.dtype), part.shape),
        value,
        identity,
    )

    def step(k, before):
        reached = k < mine
        new = combine(before, jax.tree.map(lambda part: part[k], everything))
        return jax.tree.map(lambda a, b: jnp.where(reached, a, b), new, before)

    return lax.fori_loop(0, count, step, start)


def box_valid(values):
    out_rows = values.shape[-2] - WIN_ROWS + 1
    row_sums = values[..., 0:out_rows, :]
    for offset in range(1, WIN_ROWS):
        row_sums = row_sums + values[..., offset : offset + out_rows, :]
    out_cols = values.shape[-1] - WIN_COLS + 1
    summed = row_sums[..., 0:out_cols]
    for offset in range(1, WIN_COLS):
        summed = summed + row_sums[..., offset : offset + out_cols]
    return summed


def estimate(window_block, sweep_limit):
    date_count = (window_block.shape[0] - 1) // 2
    amplitudes = window_block[:date_count]
    angles = window_block[date_count : 2 * date_count]
    weights = window_block[2 * date_count]
    real_part = amplitudes * jnp.cos(angles)
    imag_part = amplitudes * jnp.sin(angles)
    cross_real = weights * (
        real_part[:, None] * real_part[None] + imag_part[:, None] * imag_part[None]
    )
    cross_imag = weights * (
        imag_part[:, None] * real_part[None] - real_part[:, None] * imag_part[None]
    )
    power_real = box_valid(cross_real)
    power_imag = box_valid(cross_imag)
    own_power = box_valid(weights * amplitudes * amplitudes)
    inverse = 1.0 / jnp.sqrt(own_power)
    coher_real = power_real * inverse[:, None] * inverse[None]
    coher_imag = power_imag * inverse[:, None] * inverse[None]
    start_real = jnp.full(own_power.shape, 1.0 / math.sqrt(date_count), jnp.float32)
    start_imag = jnp.zeros(own_power.shape, jnp.float32)

    def power_step(turn_no, vectors):
        old_real, old_imag = vectors
        new_real = (
            jnp.sum(coher_real * old_real[None] - coher_imag * old_imag[None], axis=1) + old_real
        )
        new_imag = (
            jnp.sum(coher_real * old_imag[None] + coher_imag * old_real[None], axis=1) + old_imag
        )
        length = jnp.sqrt(jnp.sum(new_real * new_real + new_imag * new_imag, axis=0))
        active = turn_no < sweep_limit
        return (
            jnp.where(active, new_real / length, old_real),
            jnp.where(active, new_imag / length, old_imag),
        )

    vec_real, vec_imag = lax.fori_loop(0, ITERS, power_step, (start_real, start_imag))
    half_rows = WIN_ROWS // 2
    half_cols = WIN_COLS // 2
    inner_real = real_part[
        :, half_rows : real_part.shape[1] - half_rows, half_cols : real_part.shape[2] - half_cols
    ]
    inner_imag = imag_part[
        :, half_rows : imag_part.shape[1] - half_rows, half_cols : imag_part.shape[2] - half_cols
    ]
    comp_real = jnp.sum(vec_real * inner_real + vec_imag * inner_imag, axis=0)
    comp_imag = jnp.sum(vec_real * inner_imag - vec_imag * inner_real, axis=0)
    return (vec_real, vec_imag, comp_real, comp_imag)


def link_phases(stacked, sweep_limit):
    columns = stacked.shape[2]
    half_cols = WIN_COLS // 2
    padded = jnp.pad(stacked, ((0, 0), (0, 0), (half_cols, half_cols)))
    block_cols = min(128, columns)
    blocks = columns // block_cols

    def one_block(block_no):
        window = lax.dynamic_slice_in_dim(
            padded, block_no * block_cols, block_cols + 2 * half_cols, 2
        )
        return estimate(window, sweep_limit)

    results = lax.map(one_block, jnp.arange(blocks, dtype=jnp.int32))

    def merge_cols(pieces):
        placed = jnp.moveaxis(pieces, 0, -2)
        return placed.reshape(placed.shape[:-2] + (columns,))

    return tuple((merge_cols(result) for result in results))


def refer_dates(vec_real, vec_imag, chosen):
    date_count = vec_real.shape[0]
    picked = (jnp.arange(date_count, dtype=jnp.int32) == chosen).astype(jnp.float32)[:, None, None]
    ref_real = jnp.sum(vec_real * picked, axis=0)
    ref_imag = jnp.sum(vec_imag * picked, axis=0)
    linked_real = date_count * (vec_real * ref_real + vec_imag * ref_imag)
    linked_imag = date_count * (vec_imag * ref_real - vec_real * ref_imag)
    return (linked_real, linked_imag)


def pad_columns(values):
    half_cols = WIN_COLS // 2
    return jnp.pad(values, [(0, 0)] * (values.ndim - 1) + [(half_cols, half_cols)])


def link_offsets(comp_real, comp_imag, next_real, next_imag, weights):
    cross_real = box_valid(pad_columns(weights * (comp_real * next_real + comp_imag * next_imag)))
    cross_imag = box_valid(pad_columns(weights * (comp_imag * next_real - comp_real * next_imag)))
    own_power = box_valid(pad_columns(weights * (comp_real * comp_real + comp_imag * comp_imag)))
    next_power = box_valid(pad_columns(weights * (next_real * next_real + next_imag * next_imag)))
    denominator = jnp.sqrt((own_power + 1.0) * (next_power + 1.0))
    off_real = cross_real / denominator
    off_imag = cross_imag / denominator
    magnitude = jnp.sqrt(off_real * off_real + off_imag * off_imag)
    bounded = jnp.maximum(magnitude, link_floor)
    return (off_real / bounded, off_imag / bounded)


def multiply(earlier, later):
    return (
        earlier[0] * later[0] - earlier[1] * later[1],
        earlier[0] * later[1] + earlier[1] * later[0],
    )


def local(amplitude, phase, validity, iterations, reference_date):
    date_count = amplitude.shape[0]
    half_rows = WIN_ROWS // 2
    weights = jnp.where(validity == 1, 1.0, masked_weight).astype(jnp.float32)
    stacked = jnp.concatenate([amplitude, phase, weights[None]], axis=0)
    sweep_limit = iterations[0]
    chosen = reference_date[0]
    extended = extended_2(stacked, (("space", 1),), half_rows)
    vec_real, vec_imag, comp_real, comp_imag = link_phases(extended, sweep_limit)
    image_pair = jnp.stack([comp_real, comp_imag])
    following = shifted(image_pair, "tm", -1)
    image_quad = jnp.concatenate([image_pair, following], axis=0)
    margins = extended_2(image_quad, (("space", 1),), half_rows)
    unit_real, unit_imag = link_offsets(
        margins[0], margins[1], margins[2], margins[3], extended[2 * date_count]
    )
    linked_real, linked_imag = refer_dates(vec_real, vec_imag, chosen)
    datum_real, datum_imag = prefix(
        (unit_real, unit_imag),
        "tm",
        multiply,
        (jnp.ones_like(unit_real), jnp.zeros_like(unit_imag)),
    )
    out_real = linked_real * datum_real[None] - linked_imag * datum_imag[None]
    out_imag = linked_real * datum_imag[None] + linked_imag * datum_real[None]
    return jnp.stack([out_real, out_imag])


def solution(mesh):
    return jax.shard_map(
        local,
        mesh=mesh,
        in_specs=(
            P("tm", "space", None),
            P("tm", "space", None),
            P("space", None),
            P("tm"),
            P("tm"),
        ),
        out_specs=P(None, "tm", "space", None),
        check_vma=False,
    )
```

profile of v0, /device:TPU:168, one launch (start us, length us, event | category | flops | bytes accessed | tf_op | source)
XLA Modules:
  0.0 309.8 jit_solution(6308345788130480306)
XLA Ops:
  4.0 5.8 %collective-permute-start.1 = (f32[21,5,512]{2,1,0:T(8,128)S(1)}, f32[21,5,512]{2,1,0:T(8,128)S(1)}, u32[]{:S(2)}, u32[]{:S(2)}) collective-permute-start(f32[21,5,512]{2,1,0:T(8,128)S(1)} %get-tuple-element.394), channel_id=1, source_target_pairs={{1,0},{2,1},{3,2},{4,3},{5,4},{6,5},{7,6},{8,7},{9,8},{10,9},{11,1... | collective-permute-start | bytes 645128 | tf_op jit(solution)/shard_map/ppermute | solution.py:25
  19.1 175.3 %while.49 = (s32[]{:T(128)}, f32[4,10,24,128]{3,2,1,0:T(8,128)}, f32[4,10,24,128]{3,2,1,0:T(8,128)}, f32[4,24,128]{2,1,0:T(8,128)S(1)}, f32[4,24,128]{2,1,0:T(8,...) while((s32[]{:T(128)}, f32[4,10,24,128]{3,2,1,0:T(8,128)}, ...), condition=%wide.region_8.9_spmd, body=%wide.region_0.8_spmd.sunk | while | flops 17233356 | bytes 60039204 | solution.py:129
  21.3 2.7 multiply_multiply_fusion.2
  27.5 3.4 %slice_add_fusion.64 = f32[10,10,24,132]{3,2,1,0:T(8,128)} fusion(f32[10,10,34,132]{3,2,1,0:T(8,128)S(1)} %get-tuple-element.556), kind=kLoop, calls=%fused_computation.19.clone.1 | loop fusion | flops 3168000 | bytes 15206400 | tf_op jit(solution)/shard_map/while/body/eval_jaxpr/add | solution.py:57
  31.3 7.2 %fusion.61 = (f32[10,10,24,128]{3,2,1,0:T(8,128)S(1)}, f32[10,10,24,128]{3,2,1,0:T(8,128)S(1)}) fusion(f32[10,10,24,132]{3,2,1,0:T(8,128)S(1)} %slice_add_fusion.62, f32[10,24,128]{2,1,0:T(8,128)S(1)} %fusion.60, f32[10,10,24,132]{3,2,1,0:T(8,128)} %slice_add_fusion.64), kind=kLoop, calls=%fused_computation.31.clone.1 | loop fusion | flops 3686400 | bytes 14991360 | tf_op jit(solution)/shard_map/while/body/eval_jaxpr/mul | solution.py:83
  38.5 22.5 %while.51 = (s32[]{:T(128)}, f32[10,24,128]{2,1,0:T(8,128)S(1)}, f32[10,24,128]{2,1,0:T(8,128)S(1)}, s32[]{:T(128)}, f32[10,10,24,128]{3,2,1,0:T(8,128)S(1)}, /*...) while((s32[]{:T(128)}, f32[10,24,128]{2,1,0:T(8,128)S(1)}, f32[10,24,128]{2,1,0:T(8,128)S(1)}, ...), condition=%wide.region_5.5_spmd.clone, body=%wide.region_1.4_spmd.clone.sunk | while | flops 2761732 | bytes 4964457 | solution.py:102
  65.1 2.7 multiply_multiply_fusion.2
  71.3 3.4 %slice_add_fusion.64 = f32[10,10,24,132]{3,2,1,0:T(8,128)} fusion(f32[10,10,34,132]{3,2,1,0:T(8,128)S(1)} %get-tuple-element.556), kind=kLoop, calls=%fused_computation.19.clone.1 | loop fusion | flops 3168000 | bytes 15206400 | tf_op jit(solution)/shard_map/while/body/eval_jaxpr/add | solution.py:57
  75.2 7.2 %fusion.61 = (f32[10,10,24,128]{3,2,1,0:T(8,128)S(1)}, f32[10,10,24,128]{3,2,1,0:T(8,128)S(1)}) fusion(f32[10,10,24,132]{3,2,1,0:T(8,128)S(1)} %slice_add_fusion.62, f32[10,24,128]{2,1,0:T(8,128)S(1)} %fusion.60, f32[10,10,24,132]{3,2,1,0:T(8,128)} %slice_add_fusion.64), kind=kLoop, calls=%fused_computation.31.clone.1 | loop fusion | flops 3686400 | bytes 14991360 | tf_op jit(solution)/shard_map/while/body/eval_jaxpr/mul | solution.py:83
  82.4 22.5 %while.51 = (s32[]{:T(128)}, f32[10,24,128]{2,1,0:T(8,128)S(1)}, f32[10,24,128]{2,1,0:T(8,128)S(1)}, s32[]{:T(128)}, f32[10,10,24,128]{3,2,1,0:T(8,128)S(1)}, /*...) while((s32[]{:T(128)}, f32[10,24,128]{2,1,0:T(8,128)S(1)}, f32[10,24,128]{2,1,0:T(8,128)S(1)}, ...), condition=%wide.region_5.5_spmd.clone, body=%wide.region_1.4_spmd.clone.sunk | while | flops 2761732 | bytes 4964457 | solution.py:102
  109.0 2.7 multiply_multiply_fusion.2
  112.8 2.4 slice_add_fusion.62
  115.2 3.4 %slice_add_fusion.64 = f32[10,10,24,132]{3,2,1,0:T(8,128)} fusion(f32[10,10,34,132]{3,2,1,0:T(8,128)S(1)} %get-tuple-element.556), kind=kLoop, calls=%fused_computation.19.clone.1 | loop fusion | flops 3168000 | bytes 15206400 | tf_op jit(solution)/shard_map/while/body/eval_jaxpr/add | solution.py:57
  119.0 7.2 %fusion.61 = (f32[10,10,24,128]{3,2,1,0:T(8,128)S(1)}, f32[10,10,24,128]{3,2,1,0:T(8,128)S(1)}) fusion(f32[10,10,24,132]{3,2,1,0:T(8,128)S(1)} %slice_add_fusion.62, f32[10,24,128]{2,1,0:T(8,128)S(1)} %fusion.60, f32[10,10,24,132]{3,2,1,0:T(8,128)} %slice_add_fusion.64), kind=kLoop, calls=%fused_computation.31.clone.1 | loop fusion | flops 3686400 | bytes 14991360 | tf_op jit(solution)/shard_map/while/body/eval_jaxpr/mul | solution.py:83
  126.2 22.5 %while.51 = (s32[]{:T(128)}, f32[10,24,128]{2,1,0:T(8,128)S(1)}, f32[10,24,128]{2,1,0:T(8,128)S(1)}, s32[]{:T(128)}, f32[10,10,24,128]{3,2,1,0:T(8,128)S(1)}, /*...) while((s32[]{:T(128)}, f32[10,24,128]{2,1,0:T(8,128)S(1)}, f32[10,24,128]{2,1,0:T(8,128)S(1)}, ...), condition=%wide.region_5.5_spmd.clone, body=%wide.region_1.4_spmd.clone.sunk | while | flops 2761732 | bytes 4964457 | solution.py:102
  152.8 2.7 multiply_multiply_fusion.2
  158.9 3.4 %slice_add_fusion.64 = f32[10,10,24,132]{3,2,1,0:T(8,128)} fusion(f32[10,10,34,132]{3,2,1,0:T(8,128)S(1)} %get-tuple-element.556), kind=kLoop, calls=%fused_computation.19.clone.1 | loop fusion | flops 3168000 | bytes 15206400 | tf_op jit(solution)/shard_map/while/body/eval_jaxpr/add | solution.py:57
  162.8 7.2 %fusion.61 = (f32[10,10,24,128]{3,2,1,0:T(8,128)S(1)}, f32[10,10,24,128]{3,2,1,0:T(8,128)S(1)}) fusion(f32[10,10,24,132]{3,2,1,0:T(8,128)S(1)} %slice_add_fusion.62, f32[10,24,128]{2,1,0:T(8,128)S(1)} %fusion.60, f32[10,10,24,132]{3,2,1,0:T(8,128)} %slice_add_fusion.64), kind=kLoop, calls=%fused_computation.31.clone.1 | loop fusion | flops 3686400 | bytes 14991360 | tf_op jit(solution)/shard_map/while/body/eval_jaxpr/mul | solution.py:83
  170.0 22.5 %while.51 = (s32[]{:T(128)}, f32[10,24,128]{2,1,0:T(8,128)S(1)}, f32[10,24,128]{2,1,0:T(8,128)S(1)}, s32[]{:T(128)}, f32[10,10,24,128]{3,2,1,0:T(8,128)S(1)}, /*...) while((s32[]{:T(128)}, f32[10,24,128]{2,1,0:T(8,128)S(1)}, f32[10,24,128]{2,1,0:T(8,128)S(1)}, ...), condition=%wide.region_5.5_spmd.clone, body=%wide.region_1.4_spmd.clone.sunk | while | flops 2761732 | bytes 4964457 | solution.py:102
  194.6 2.5 collective-permute-start.2
  198.4 2.8 collective-permute-done.2
  203.2 5.8 %collective-permute-start.4 = (f32[4,5,512]{2,1,0:T(8,128)S(1)}, f32[4,5,512]{2,1,0:T(8,128)S(1)}, u32[]{:S(2)}, u32[]{:S(2)}) collective-permute-start(f32[4,5,512]{2,1,0:T(8,128)S(1)} %get-tuple-element.396), channel_id=1, source_target_pairs={{1,0},{2,1},{3,2},{4,3},{5,4},{6,5},{7,6},{8,7},{9,8},{10,9},{11,1... | collective-permute-start | bytes 122888 | tf_op jit(solution)/shard_map/ppermute | solution.py:25
  213.0 45.5 %all-gather = f32[384,512]{1,0:T(8,128)S(1)} all-gather(f32[24,512]{1,0:T(8,128)S(1)} %div.47), channel_id=2, replica_groups=mesh['tm'=16,'space'=16] {'tm'}, dimensions={0}, use_global_device_ids=true | all-gather | bytes 835584 | tf_op jit(solution)/shard_map/all_gather | solution.py:38
  258.5 49.2 %all-gather.1 = f32[384,512]{1,0:T(8,128)S(1)} all-gather(f32[24,512]{1,0:T(8,128)S(1)} %get-tuple-element.367), channel_id=3, replica_groups=mesh['tm'=16,'space'=16] {'tm'}, dimensions={0}, use_global_device_ids=true | all-gather | bytes 835584 | tf_op jit(solution)/shard_map/all_gather | solution.py:38
  (531 shorter events, 84.4 us)
Async XLA Ops:
  2.0 10.7 %collective-permute-start = (f32[21,5,512]{2,1,0:T(8,128)S(1)}, f32[21,5,512]{2,1,0:T(8,128)S(1)}, u32[]{:S(2)}, u32[]{:S(2)}) collective-permute-start(f32[21,5,512]{2,1,0:T(8,128)S(1)} %get-tuple-element.393), channel_id=1, source_target_pairs={{0,1},{1,2},{2,3},{3,4},{4,5},{5,6},{6,7},{7,8},{8,9},{9,10},{10,1... | collective-permute-start | bytes 645128 | tf_op jit(solution)/shard_map/ppermute | solution.py:24
  4.0 10.5 %collective-permute-start.1 = (f32[21,5,512]{2,1,0:T(8,128)S(1)}, f32[21,5,512]{2,1,0:T(8,128)S(1)}, u32[]{:S(2)}, u32[]{:S(2)}) collective-permute-start(f32[21,5,512]{2,1,0:T(8,128)S(1)} %get-tuple-element.394), channel_id=1, source_target_pairs={{1,0},{2,1},{3,2},{4,3},{5,4},{6,5},{7,6},{8,7},{9,8},{10,9},{11,1... | collective-permute-start | bytes 645128 | tf_op jit(solution)/shard_map/ppermute | solution.py:25
  15.9 1.3 copy-start.2
  19.1 177.9 %copy-start.7 = (f32[10]{0:T(128)S(1)}, f32[10]{0:T(128)}, u32[]{:S(2)}) copy-start(f32[10]{0:T(128)} %compare_convert_fusion) | copy-start | bytes 124
  24.0 1.1 copy-start
  24.0 1.1 copy-start.1
  67.9 1.1 copy-start
  67.9 1.1 copy-start.1
  111.7 1.1 copy-start
  111.7 1.1 copy-start.1
  155.5 1.1 copy-start
  155.5 1.1 copy-start.1
  194.5 14.5 %copy-start.3 = (f32[4,10,24,128]{3,2,1,0:T(8,128)S(1)}, f32[4,10,24,128]{3,2,1,0:T(8,128)}, u32[]{:S(2)}) copy-start(f32[4,10,24,128]{3,2,1,0:T(8,128)} %get-tuple-element.270) | copy-start | bytes 1474564
  194.5 14.9 %copy-start.4 = (f32[4,10,24,128]{3,2,1,0:T(8,128)S(1)}, f32[4,10,24,128]{3,2,1,0:T(8,128)}, u32[]{:S(2)}) copy-start(f32[4,10,24,128]{3,2,1,0:T(8,128)} %get-tuple-element.271) | copy-start | bytes 1474564
  194.6 6.6 %collective-permute-start.2 = (f32[2,24,512]{2,1,0:T(8,128)S(1)}, f32[2,24,512]{2,1,0:T(8,128)S(1)}, u32[]{:S(2)}, u32[]{:S(2)}) collective-permute-start(f32[2,24,512]{2,1,0:T(8,128)S(1)} %pad_maximum_fusion.6), channel_id=1, source_target_pairs={{16,0},{32,16},{48,32},{64,48},{80,64},{96,80},{112,96},{128,112},... | collective-permute-start | bytes 294920 | tf_op jit(solution)/shard_map/ppermute | solution.py:33
  201.3 8.6 %collective-permute-start.3 = (f32[4,5,512]{2,1,0:T(8,128)S(1)}, f32[4,5,512]{2,1,0:T(8,128)S(1)}, u32[]{:S(2)}, u32[]{:S(2)}) collective-permute-start(f32[4,5,512]{2,1,0:T(8,128)S(1)} %get-tuple-element.395), channel_id=1, source_target_pairs={{0,1},{1,2},{2,3},{3,4},{4,5},{5,6},{6,7},{7,8},{8,9},{9,10},{10,1... | collective-permute-start | bytes 122888 | tf_op jit(solution)/shard_map/ppermute | solution.py:24
  203.2 7.6 %collective-permute-start.4 = (f32[4,5,512]{2,1,0:T(8,128)S(1)}, f32[4,5,512]{2,1,0:T(8,128)S(1)}, u32[]{:S(2)}, u32[]{:S(2)}) collective-permute-start(f32[4,5,512]{2,1,0:T(8,128)S(1)} %get-tuple-element.396), channel_id=1, source_target_pairs={{1,0},{2,1},{3,2},{4,3},{5,4},{6,5},{7,6},{8,7},{9,8},{10,9},{11,1... | collective-permute-start | bytes 122888 | tf_op jit(solution)/shard_map/ppermute | solution.py:25
  209.8 97.8 %copy-start.5 = (f32[24,512]{1,0:T(8,128)S(1)}, f32[24,512]{1,0:T(8,128)}, u32[]{:S(2)}) copy-start(f32[24,512]{1,0:T(8,128)} %custom-call.2) | copy-start | bytes 147460
  209.8 97.8 %copy-start.6 = (f32[24,512]{1,0:T(8,128)S(1)}, f32[24,512]{1,0:T(8,128)}, u32[]{:S(2)}) copy-start(f32[24,512]{1,0:T(8,128)} %custom-call.3) | copy-start | bytes 147460
where the time goes:
time: 311 us; the launch traced here: 310 us
  other arithmetic  117 us (38%)
  blocking collectives  94.6 us (30%)
  loops' own time  58.3 us (19%)
  starting transfers between devices  17.8 us (6%)
  local copies, waits for them, and re-layouts  13.9 us (4%)
  waiting for transfers between devices  7.26 us (2%)
    all_gather x2, blocking collectives, prefix(): everything = jax.tree.map(lambda part: lax.all_gather(part, axis), value)  94.6 us
    another operation x4, loops' own time, estimate(): lax.fori_loop(0, ITERS, power_step, (start_real, start_imag))  55 us
    mul x4, other arithmetic, estimate(): coher_imag = power_imag * inverse[:, None] * inverse[None]  28.6 us
    reduce_sum x80, other arithmetic, power_step(): jnp.sum(coher_real * old_imag[None] + coher_imag * old_real[None], axis=1)  25.8 us
    add x14, other arithmetic, box_valid(): row_sums = row_sums + values[..., offset:offset + out_rows, :]  25 us
    ppermute x2, starting transfers between devices, extended_2(): after = lax.ppermute(leading, axis, down)  11.5 us
    mul x4, other arithmetic, estimate(): own_power = box_valid(weights * amplitudes * amplitudes)  10.8 us
  transfers between devices with their start and end apart: 5, of which 4 were waited for; matrix products, arithmetic and copies ran while one was open for 1% of the time, Pallas kernels for 0%

commit v1 on v0

v1 whole, which is shorter than its diff:
```python
import jax
import jax.numpy as jnp
from jax import lax
from jax.experimental import pallas as pl
from jax.experimental.pallas import tpu as pltpu
from jax.sharding import PartitionSpec as P

MESH = pl.DeviceIdType.MESH
DATES = 10
REACH = 5
FOLD = 12
EXT = FOLD + 2 * REACH
ROWS = 2 * FOLD
TILES = ROWS // 8
MASKED = 0.125
FLOOR = 0.03
F32 = jnp.float32

SIN = (1.0, -1.0 / 6, 1.0 / 120, -1.0 / 5040, 1.0 / 362880, -1.0 / 39916800)
COS = (1.0, -1.0 / 2, 1.0 / 24, -1.0 / 720, 1.0 / 40320, -1.0 / 3628800, 1.0 / 479001600)


def horner(terms, x):
    total = terms[-1] * x + terms[-2]
    for term in terms[-3::-1]:
        total = total * x + term
    return total


def phasor(amplitude, phase):
    half = 0.5 * phase
    square = half * half
    sine = horner(SIN, square) * half
    cosine = horner(COS, square)
    twice = sine + sine
    return amplitude - amplitude * (twice * sine), amplitude * (twice * cosine)


def sublanes():
    return lax.broadcasted_iota(jnp.int32, (8, 128), 0)


def lanes():
    return lax.broadcasted_iota(jnp.int32, (8, 128), 1)


def column_sum():
    lane, block = lanes(), sublanes() & 3
    not_first = jnp.where(block > 0, 1.0, 0.0).astype(F32)
    not_last = jnp.where(block < 3, 1.0, 0.0).astype(F32)
    edges = [(amount, lane >= 128 - amount, lane < amount) for amount in (1, 2)]

    def apply(x):
        before = pltpu.roll(x, 1, 0) * not_first
        after = pltpu.roll(x, 7, 0) * not_last
        total = x
        for amount, high, low in edges:
            total = total + pltpu.roll(jnp.where(high, before, x), amount, 1)
            total = total + pltpu.roll(jnp.where(low, after, x), 128 - amount, 1)
        return total

    return apply


def row_sums(values):
    tails = [None] * 11
    tails[10] = values[10]
    for r in range(9, -1, -1):
        tails[r] = tails[r + 1] + values[r]
    out = [tails[0]]
    head = values[11]
    for r in range(1, 11):
        out.append(tails[r] + head)
        head = head + values[r + 11]
    out.append(head)
    return out


def halo_kernel(amp, pha, val, zr, zi, wt, A, B, V, local, send, recv):
    count = lax.axis_size("space")
    me = lax.axis_index("space")
    up, down = lax.rem(me + count - 1, count), lax.rem(me + 1, count)
    arrays = ((amp, A), (pha, B), (val, V))

    def lead(source):
        return (slice(None),) * (len(source.shape) - 4)

    for k, (source, target) in enumerate(arrays):
        all_ = lead(source)
        for r in range(FOLD + REACH):
            for half, row in ((0, r), (1, ROWS - 1 - r)):
                pltpu.make_async_copy(
                    source.at[all_ + (row // 8, slice(None), row % 8)],
                    target.at[all_ + (REACH + r, pl.ds(4 * half, 4))],
                    local.at[k],
                ).start()

    barrier = pltpu.get_barrier_semaphore()
    for neighbour in (up, down):
        pl.semaphore_signal(barrier, inc=1, device_id={"space": neighbour}, device_id_type=MESH)
    pl.semaphore_wait(barrier, 2)

    for k, (source, target) in enumerate(arrays):
        all_ = lead(source)
        for r in range(REACH):
            for half, row, to in ((0, ROWS - 1 - r, down), (1, r, up)):
                pltpu.make_async_remote_copy(
                    source.at[all_ + (row // 8, slice(None), row % 8)],
                    target.at[all_ + (REACH - 1 - r, pl.ds(4 * half, 4))],
                    send.at[k, half],
                    recv.at[k, half],
                    device_id={"space": to},
                    device_id_type=MESH,
                ).start()

    for k, (source, target) in enumerate(arrays):
        own = target.at[lead(source) + (pl.ds(REACH, FOLD + REACH),)]
        pltpu.make_async_copy(own, own, local.at[k]).wait()

    def phasors(first, last):
        def one(d, carry):
            for p in range(first, last):
                real, imag = phasor(A[d, p], B[d, p])
                zr[d, p] = real
                zi[d, p] = imag
            return carry

        lax.fori_loop(0, DATES, one, 0)

    phasors(REACH, EXT)
    for p in range(REACH, EXT):
        wt[p] = jnp.where(V[p] == 1, 1.0, MASKED).astype(F32)

    for k, (source, target) in enumerate(arrays):
        for half in range(2):
            edge = target.at[lead(source) + (pl.ds(0, REACH), pl.ds(4 * half, 4))]
            pltpu.make_async_copy(edge, edge, send.at[k, half]).wait()
            pltpu.make_async_copy(edge, edge, recv.at[k, half]).wait()

    phasors(0, REACH)
    above = jnp.where(me > 0, 1.0, 0.0).astype(F32)
    below = jnp.where(me < count - 1, 1.0, 0.0).astype(F32)
    inside = jnp.where(sublanes() < 4, above, below)
    for p in range(REACH):
        wt[p] = jnp.where(V[p] == 1, 1.0, MASKED).astype(F32) * inside


def main_kernel(iterations, chosen, zr, zi, wt, linked, comp, wr, wi, inv, R, I, S, QR, QI, QS, QD, vec):
    columns = column_sum()

    def own_power(d, carry):
        values = [wt[p] * (zr[d, p] * zr[d, p] + zi[d, p] * zi[d, p]) for p in range(EXT)]
        for r, total in enumerate(row_sums(values)):
            inv[d, r] = 0.5 * lax.rsqrt(columns(total))
        return carry

    lax.fori_loop(0, DATES, own_power, 0)

    def first_date(i, carry):
        for p in range(EXT):
            wr[p] = wt[p] * zr[i, p]
            wi[p] = wt[p] * zi[i, p]

        def second_date(j, carry):
            real, imag = [], []
            for p in range(EXT):
                a, b, c, d = wr[p], wi[p], zr[j, p], zi[j, p]
                real.append(a * c + b * d)
                imag.append(b * c - a * d)
            real, imag = row_sums(real), row_sums(imag)
            for r in range(FOLD):
                scale = inv[i, r] * inv[j, r]
                x = columns(real[r]) * scale
                y = columns(imag[r]) * scale
                R[r, i * DATES + j] = x
                I[r, i * DATES + j] = y
                S[r, i * DATES + j] = x + y
                S[r, j * DATES + i] = x - y
            return carry

        return lax.fori_loop(i + 1, DATES, second_date, carry)

    lax.fori_loop(0, DATES - 1, first_date, 0)

    n = iterations[0]
    odd = (n & 1) == 1
    turns = (n - 1) >> 1
    ref = chosen[0]

    def flat(i, j):
        return i * DATES + j

    def upper(i, j):
        return flat(min(i, j), max(i, j))

    def row_total(real, imag, diagonal):
        out_r, out_i = [], []
        for i in range(DATES):
            tr, ti = diagonal(i), None
            for j in range(DATES):
                if j == i:
                    continue
                tr = tr + real(upper(i, j))
                value = imag(upper(i, j))
                if ti is None:
                    ti = value if i < j else -value
                else:
                    ti = ti + value if i < j else ti - value
            out_r.append(tr)
            out_i.append(ti)
        return out_r, out_i

    def position(r, carry):
        squares = [jnp.full((8, 128), 0.25, F32) for _ in range(DATES)]
        for i in range(DATES):
            for j in range(i + 1, DATES):
                k = flat(i, j)
                x, y = R[r, k], I[r, k]
                size = x * x + y * y
                squares[i] = squares[i] + size
                squares[j] = squares[j] + size
        for i in range(DATES):
            QD[i] = squares[i]
        for i in range(DATES):
            for j in range(i + 1, DATES):
                rr, ii, mixed = None, None, None
                for k in range(DATES):
                    if k == i or k == j:
                        continue
                    a = R[r, upper(i, k)] * R[r, upper(j, k)]
                    b = I[r, upper(i, k)] * I[r, upper(j, k)]
                    c = S[r, flat(i, k)] * S[r, flat(k, j)]
                    same = (i < k) == (j < k)
                    rr = a if rr is None else rr + a
                    if ii is None:
                        ii = b if same else -b
                    else:
                        ii = ii + b if same else ii - b
                    mixed = c if mixed is None else mixed + c
                k = flat(i, j)
                x = R[r, k] + (rr + ii)
                y = I[r, k] + (mixed - (rr - ii))
                QR[k] = x
                QI[k] = y
                QS[k] = x + y
                QS[flat(j, i)] = x - y

        one_r, one_i = row_total(lambda k: R[r, k], lambda k: I[r, k], lambda i: jnp.full((8, 128), 0.5, F32))
        two_r, two_i = row_total(lambda k: QR[k], lambda k: QI[k], lambda i: QD[i])
        start = [jnp.where(odd, a, b) for a, b in zip(one_r + one_i, two_r + two_i)]

        def turn(_, v):
            vr, vi = v[:DATES], v[DATES:]
            both = [a + b for a, b in zip(vr, vi)]
            out_r, out_i = [], []
            for i in range(DATES):
                d = QD[i]
                rr, ii, mixed = None, None, None
                for j in range(DATES):
                    if j == i:
                        continue
                    a = QR[upper(i, j)] * vr[j]
                    b = QI[upper(i, j)] * vi[j]
                    c = QS[flat(i, j)] * both[j]
                    rr = a if rr is None else rr + a
                    if ii is None:
                        ii = b if i < j else -b
                    else:
                        ii = ii + b if i < j else ii - b
                    mixed = c if mixed is None else mixed + c
                out_r.append(d * vr[i] + (rr - ii))
                out_i.append(d * vi[i] + (mixed - (rr + ii)))
            return out_r + out_i

        v = lax.fori_loop(0, turns, turn, start)
        total = None
        for x in v:
            total = x * x if total is None else total + x * x
        scale = lax.rsqrt(total)
        v = [x * scale for x in v]
        vr, vi = v[:DATES], v[DATES:]
        for t in range(2 * DATES):
            vec[t] = v[t]
        cr, ci = None, None
        for t in range(DATES):
            a, b = zr[t, r + REACH], zi[t, r + REACH]
            x = vr[t] * a + vi[t] * b
            y = vr[t] * b - vi[t] * a
            cr = x if cr is None else cr + x
            ci = y if ci is None else ci + y
        comp[0, r] = cr
        comp[1, r] = ci
        ref_r, ref_i = DATES * vec[ref], DATES * vec[DATES + ref]
        for t in range(DATES):
            x = vr[t] * ref_r + vi[t] * ref_i
            y = vi[t] * ref_r - vr[t] * ref_i
            for part, value in ((t, x), (DATES + t, y)):
                for half, row in ((0, r), (1, ROWS - 1 - r)):
                    first = (row >> 3) * 32 + (row & 7)
                    linked[part, pl.ds(first, 4, stride=8), :] = value[4 * half : 4 * half + 4]
        return carry

    lax.fori_loop(0, FOLD, position, 0)


def link_kernel(comp, wt, datum, near, own_edge, near_edge, u, got, ready, dat, sem, send_u, recv_u, send_d, recv_d):
    stacks, spaces = lax.axis_size("tm"), lax.axis_size("space")
    m, s = lax.axis_index("tm"), lax.axis_index("space")
    before, after = lax.rem(m + stacks - 1, stacks), lax.rem(m + 1, stacks)
    up, down = lax.rem(s + spaces - 1, spaces), lax.rem(s + 1, spaces)

    barrier = pltpu.get_barrier_semaphore()

    def greet(tm, space):
        pl.semaphore_signal(barrier, inc=1, device_id={"tm": tm, "space": space}, device_id_type=MESH)

    for step in range(1, stacks):
        greet(lax.rem(m + step, stacks), s)
    for space in (up, down):
        greet(m, space)
        greet(before, space)
        greet(after, space)
    pl.semaphore_wait(barrier, stacks - 1 + 6)

    heads, tails = pl.ds(0, 4), pl.ds(4, 4)
    edge = pl.ds(0, REACH)
    plan = (
        (comp, near, (before, s)),
        (comp.at[:, edge, tails], own_edge.at[:, :, heads], (m, down)),
        (comp.at[:, edge, heads], own_edge.at[:, :, tails], (m, up)),
        (comp.at[:, edge, tails], near_edge.at[:, :, heads], (before, down)),
        (comp.at[:, edge, heads], near_edge.at[:, :, tails], (before, up)),
    )
    copies = []
    for k, (source, target, (tm, space)) in enumerate(plan):
        copy = pltpu.make_async_remote_copy(
            source, target, sem.at[0, k], sem.at[1, k], device_id={"tm": tm, "space": space}, device_id_type=MESH
        )
        copy.start()
        copies.append(copy)
    for copy in copies:
        copy.wait()

    def extended(block, edges, part):
        rows = [edges[part, REACH - 1 - k] for k in range(REACH)]
        rows += [block[part, r] for r in range(FOLD)]
        rows += [pltpu.roll(block[part, FOLD - 1 - k], 4, 0) for k in range(REACH)]
        return rows

    ar, ai = extended(comp, own_edge, 0), extended(comp, own_edge, 1)
    br, bi = extended(near, near_edge, 0), extended(near, near_edge, 1)
    columns = column_sum()
    cross_r, cross_i, power_a, power_b = [], [], [], []
    for p in range(EXT):
        w = wt[p]
        xr, xi = w * ar[p], w * ai[p]
        cross_r.append(xr * br[p] + xi * bi[p])
        cross_i.append(xi * br[p] - xr * bi[p])
        power_a.append(xr * ar[p] + xi * ai[p])
        power_b.append(w * (br[p] * br[p] + bi[p] * bi[p]))
    cross_r, cross_i, power_a, power_b = [row_sums(x) for x in (cross_r, cross_i, power_a, power_b)]
    for r in range(FOLD):
        scale = lax.rsqrt((columns(power_a[r]) + 1.0) * (columns(power_b[r]) + 1.0))
        x, y = columns(cross_r[r]) * scale, columns(cross_i[r]) * scale
        bounded = lax.rsqrt(jnp.maximum(x * x + y * y, FLOOR * FLOOR))
        u[r, 0] = x * bounded
        u[r, 1] = y * bounded

    def u_copy(step):
        to = lax.rem(m + step, stacks)
        return to, pltpu.make_async_remote_copy(
            u.at[to], got.at[m], send_u.at[to], recv_u.at[m], device_id={"tm": to}, device_id_type=MESH
        )

    for step in range(1, stacks):
        to = lax.rem(m + step, stacks)

        @pl.when(to < FOLD)
        def _():
            u_copy(step)[1].start()

    @pl.when(m < FOLD)
    def _():
        got[m] = u[m]
        xr, xi = jnp.ones((8, 128), F32), jnp.zeros((8, 128), F32)
        for k in range(stacks):
            ready[k, 0] = xr
            ready[k, 1] = xi

            @pl.when(k != m)
            def _():
                pltpu.make_async_remote_copy(
                    ready.at[k], dat.at[m], send_d.at[k], recv_d.at[m], device_id={"tm": k}, device_id_type=MESH
                ).start()

            @pl.when(k != m)
            def _():
                pltpu.make_async_copy(got.at[k], got.at[k], recv_u.at[k]).wait()

            lr, li = got[k, 0], got[k, 1]
            xr, xi = xr * lr - xi * li, xr * li + xi * lr
        dat[m] = ready[m]

    for r in range(FOLD):

        @pl.when(r != m)
        def _():
            pltpu.make_async_copy(dat.at[r], dat.at[r], recv_d.at[r]).wait()
            pltpu.make_async_copy(u.at[r], u.at[r], send_u.at[r]).wait()

    for r in range(FOLD):
        for part in range(2):
            value = dat[r, part]
            for half, row in ((0, r), (1, ROWS - 1 - r)):
                datum[part, pl.ds((row // 8) * 32 + row % 8, 4, stride=8), :] = value[4 * half : 4 * half + 4]

    @pl.when(m < FOLD)
    def _():
        for k in range(stacks):

            @pl.when(k != m)
            def _():
                pltpu.make_async_copy(ready.at[k], ready.at[k], send_d.at[k]).wait()


def vmem():
    return pl.BlockSpec(memory_space=pltpu.VMEM)


def smem():
    return pl.BlockSpec(memory_space=pltpu.SMEM)


def anywhere():
    return pl.BlockSpec(memory_space=pl.ANY)


def shape(*dims):
    return jax.ShapeDtypeStruct(dims, F32)


def scratch(*dims):
    return pltpu.VMEM(dims, F32)


def tiled(x):
    lead = x.shape[:-2]
    k = len(lead)
    return x.reshape(lead + (TILES, 8, 4, 128)).transpose(tuple(range(k)) + (k, k + 2, k + 1, k + 3))


def local(amplitude, phase, validity, iterations, reference_date):
    dma = pltpu.SemaphoreType.DMA
    zr, zi, wt = pl.pallas_call(
        halo_kernel,
        out_shape=[shape(DATES, EXT, 8, 128), shape(DATES, EXT, 8, 128), shape(EXT, 8, 128)],
        in_specs=[anywhere()] * 3,
        out_specs=[vmem()] * 3,
        scratch_shapes=[
            scratch(DATES, EXT, 8, 128),
            scratch(DATES, EXT, 8, 128),
            pltpu.VMEM((EXT, 8, 128), jnp.int32),
            dma((3,)),
            dma((3, 2)),
            dma((3, 2)),
        ],
        compiler_params=pltpu.CompilerParams(
            collective_id=0, has_side_effects=True, vmem_limit_bytes=16 << 20
        ),
        name="halo",
    )(tiled(amplitude), tiled(phase), tiled(validity))
    linked, comp = pl.pallas_call(
        main_kernel,
        out_shape=[shape(2 * DATES, 4 * ROWS, 128), shape(2, FOLD, 8, 128)],
        in_specs=[smem(), smem(), vmem(), vmem(), vmem()],
        out_specs=[vmem(), vmem()],
        scratch_shapes=[
            scratch(EXT, 8, 128),
            scratch(EXT, 8, 128),
            scratch(DATES, FOLD, 8, 128),
            scratch(FOLD, DATES * DATES, 8, 128),
            scratch(FOLD, DATES * DATES, 8, 128),
            scratch(FOLD, DATES * DATES, 8, 128),
            scratch(DATES * DATES, 8, 128),
            scratch(DATES * DATES, 8, 128),
            scratch(DATES * DATES, 8, 128),
            scratch(DATES, 8, 128),
            scratch(2 * DATES, 8, 128),
        ],
        compiler_params=pltpu.CompilerParams(vmem_limit_bytes=40 << 20),
        name="power",
    )(iterations, reference_date, zr, zi, wt)
    datum = pl.pallas_call(
        link_kernel,
        out_shape=shape(2, 4 * ROWS, 128),
        in_specs=[vmem(), vmem()],
        out_specs=vmem(),
        scratch_shapes=[
            scratch(2, FOLD, 8, 128),
            scratch(2, REACH, 8, 128),
            scratch(2, REACH, 8, 128),
            scratch(16, 2, 8, 128),
            scratch(16, 2, 8, 128),
            scratch(16, 2, 8, 128),
            scratch(16, 2, 8, 128),
            dma((2, 5)),
            dma((16,)),
            dma((16,)),
            dma((16,)),
            dma((16,)),
        ],
        compiler_params=pltpu.CompilerParams(
            collective_id=1, has_side_effects=True, vmem_limit_bytes=16 << 20
        ),
        name="links",
    )(comp, wt)
    lr, li = linked[:DATES], linked[DATES:]
    dr, di = datum[0], datum[1]
    out = jnp.stack([lr * dr - li * di, lr * di + li * dr])
    out = out.reshape(2, DATES, TILES, 4, 8, 128).transpose(0, 1, 2, 4, 3, 5)
    return out.reshape(2, DATES, ROWS, 512)


def solution(mesh):
    return jax.shard_map(
        local,
        mesh=mesh,
        in_specs=(P("tm", "space", None), P("tm", "space", None), P("space", None), P("tm"), P("tm")),
        out_specs=P(None, "tm", "space", None),
        check_vma=False,
    )
```

time: 311 us -> 70.7 us (0.23)
  the two profiles are of different devices: /device:TPU:168 before, /device:TPU:64 now
where the time goes in v1:
time: 70.7 us; the launch traced here: 70.5 us
  Pallas kernels  65.2 us (92%)
  local copies, waits for them, and re-layouts  2.86 us (4%)
  between operations  1.35 us (2%)
  other arithmetic  1.15 us (2%)
    pallas_call x1, Pallas kernels, local(): pl.pallas_call(link_kernel, out_shape=shape(2, 4 * ROWS, 128), in_specs=[...  34.8 us
    pallas_call x1, Pallas kernels, local(): pl.pallas_call(main_kernel, out_shape=[shape(2 * DATES, 4 * ROWS, 128), s...  21 us
    pallas_call x1, Pallas kernels, local(): pl.pallas_call(halo_kernel, out_shape=[shape(DATES, EXT, 8, 128), shape(D...  9.36 us
    unnamed x6, local copies, waits for them, and re-layouts  2.85 us

profile of v1, /device:TPU:64, one launch (start us, length us, event | category | flops | bytes accessed | tf_op | source)
XLA Modules:
  0.0 70.5 jit_solution(7541456354395284720)
XLA Ops:
  1.3 0.0 copy-start
  1.3 1.0 %copy-done = f32[10,24,512]{2,1,0:T(8,128)S(1)} copy-done((f32[10,24,512]{2,1,0:T(8,128)S(1)}, f32[10,24,512]{2,1,0:T(8,128)}, u32[]{:S(2)}) %copy-start) | copy-done | bytes 491544
  2.3 0.0 copy-start.1
  2.3 1.0 %copy-done.1 = f32[10,24,512]{2,1,0:T(8,128)S(1)} copy-done((f32[10,24,512]{2,1,0:T(8,128)S(1)}, f32[10,24,512]{2,1,0:T(8,128)}, u32[]{:S(2)}) %copy-start.1) | copy-done | bytes 491544
  3.4 0.0 copy-start.2
  3.4 0.8 %copy-done.2 = s32[24,512]{1,0:T(8,128)S(1)} copy-done((s32[24,512]{1,0:T(8,128)S(1)}, s32[24,512]{1,0:T(8,128)}, u32[]{:S(2)}) %copy-start.2) | copy-done | bytes 49176
  4.2 9.4 %halo.1 = (f32[10,22,8,128]{3,2,1,0:T(8,128)S(1)}, f32[10,22,8,128]{3,2,1,0:T(8,128)S(1)}, f32[22,8,128]{2,1,0:T(8,128)S(1)}) custom-call(f32[10,3,4,8,128]{4,3,2,1,0:T(8,128)S(1)} %bitcast.19, f32[10,3,4,8,128]{4,3,2,1,0:T(8,128)S(1)} %bitcast.20, s32[3,4,8,128]{3,2,1,0:T(8,128)S(1)} %bitcast.21), custom_call_target="tpu_custom_call" | custom-call | tf_op jit(solution)/shard_map/halo/pallas_call | solution.py:454
  13.5 21.0 %power.1 = (f32[20,96,128]{2,1,0:T(8,128)S(1)}, f32[2,12,8,128]{3,2,1,0:T(8,128)S(1)}) custom-call(s32[1]{0:T(128)S(6)} %copy.6.iterations, s32[1]{0:T(128)S(6)} %copy.7.chosen, f32[10,22,8,128]{3,2,1,0:T(8,128)S(1)} %get-tuple-element.10.zr, f32[10,22,8,128]{3,2,1,0:T(8,128)S(1)} %get-tuple-element.11.zi, f32[22,8,128]{2,1,0:T(8,128)S(1)} %get-tuple-element.12.wt), custom_call_target="tpu_custom_call" | custom-call | tf_op jit(solution)/shard_map/power/pallas_call | solution.py:472
  34.5 34.8 %links.1 = f32[2,96,128]{2,1,0:T(8,128)S(1)} custom-call(f32[2,12,8,128]{3,2,1,0:T(8,128)S(1)} %get-tuple-element.14.comp, f32[22,8,128]{2,1,0:T(8,128)S(1)} %get-tuple-element.12.wt), custom_call_target="tpu_custom_call" | custom-call | tf_op jit(solution)/shard_map/links/pallas_call | solution.py:493
  69.4 0.1 multiply_subtract_fusion
  69.5 1.0 %maximum_bitcast_fusion = f32[2,10,24,512]{3,2,1,0:T(8,128)} fusion(f32[1,10,3,4,8,128]{5,4,3,2,1,0:T(8,128)S(1)} %bitcast.23, f32[1,10,3,4,8,128]{5,4,3,2,1,0:T(8,128)S(1)} %bitcast.22), kind=kLoop, calls=%fused_computation | loop fusion | flops 245760 | bytes 1966080 | tf_op jit(solution)/shard_map/reshape | solution.py:521
  (1 shorter events, 0.0 us)
Async XLA Ops:
  1.3 1.0 %copy-start = (f32[10,24,512]{2,1,0:T(8,128)S(1)}, f32[10,24,512]{2,1,0:T(8,128)}, u32[]{:S(2)}) copy-start(f32[10,24,512]{2,1,0:T(8,128)} %param.5) | copy-start | bytes 1474564
  2.3 1.0 %copy-start.1 = (f32[10,24,512]{2,1,0:T(8,128)S(1)}, f32[10,24,512]{2,1,0:T(8,128)}, u32[]{:S(2)}) copy-start(f32[10,24,512]{2,1,0:T(8,128)} %param.6) | copy-start | bytes 1474564
  3.4 0.8 %copy-start.2 = (s32[24,512]{1,0:T(8,128)S(1)}, s32[24,512]{1,0:T(8,128)}, u32[]{:S(2)}) copy-start(s32[24,512]{1,0:T(8,128)} %param.7) | copy-start | bytes 147460

commit v2 on v1

--- a/solution.py
+++ b/solution.py
@@ -58,6 +58,38 @@
             total = total + pltpu.roll(jnp.where(high, before, x), amount, 1)
             total = total + pltpu.roll(jnp.where(low, after, x), 128 - amount, 1)
         return total
+
+    return apply
+
+
+def band_matrix():
+    k = lax.broadcasted_iota(jnp.int32, (256, 256), 0) & 127
+    n = lax.broadcasted_iota(jnp.int32, (256, 256), 1)
+    to = n & 127
+    own = (n < 128) & (jnp.abs(k - to) <= 2)
+    to_next = (n >= 128) & (to < 64) & (k - 128 >= to - 2)
+    to_previous = (n >= 128) & (to >= 64) & (k + 128 <= to + 2)
+    return jnp.where(own | to_next | to_previous, 1.0, 0.0).astype(jnp.bfloat16)
+
+
+def column_sums(band, spill):
+    lane, block = lanes(), sublanes() & 3
+    from_previous = (lane < 64) & (block > 0)
+    from_next = (lane >= 64) & (block < 3)
+
+    def apply(values, slot):
+        x = jnp.concatenate(values, axis=0)
+        lead = x.astype(jnp.bfloat16)
+        rest = (x - lead.astype(F32)).astype(jnp.bfloat16)
+        sums = jnp.dot(jnp.concatenate([lead, rest], axis=1), band[...], preferred_element_type=F32)
+        spill[slot, pl.ds(8, 8 * len(values))] = sums[:, 128:]
+        out = []
+        for k in range(len(values)):
+            total = sums[8 * k : 8 * k + 8, :128]
+            total = total + jnp.where(from_previous, spill[slot, pl.ds(8 * k + 7, 8)], 0.0)
+            total = total + jnp.where(from_next, spill[slot, pl.ds(8 * k + 9, 8)], 0.0)
+            out.append(total)
+        return out
 
     return apply
 
@@ -145,42 +177,50 @@
         wt[p] = jnp.where(V[p] == 1, 1.0, MASKED).astype(F32) * inside
 
 
-def main_kernel(iterations, chosen, zr, zi, wt, linked, comp, wr, wi, inv, R, I, S, QR, QI, QS, QD, vec):
-    columns = column_sum()
-
-    def own_power(d, carry):
-        values = [wt[p] * (zr[d, p] * zr[d, p] + zi[d, p] * zi[d, p]) for p in range(EXT)]
-        for r, total in enumerate(row_sums(values)):
-            inv[d, r] = 0.5 * lax.rsqrt(columns(total))
+def main_kernel(iterations, chosen, zr, zi, wt, linked, comp, wr, wi, inv, R, I, S, QR, QI, QS, QD, vec, band, spill):
+    band[...] = band_matrix()
+    columns = column_sums(band, spill)
+
+    def own_power(k, carry):
+        for t in range(2):
+            d = 2 * k + t
+            values = [wt[p] * (zr[d, p] * zr[d, p] + zi[d, p] * zi[d, p]) for p in range(EXT)]
+            for r, total in enumerate(columns(row_sums(values), t)):
+                inv[d, r] = 0.5 * lax.rsqrt(total)
         return carry
 
-    lax.fori_loop(0, DATES, own_power, 0)
-
-    def first_date(i, carry):
+    lax.fori_loop(0, DATES // 2, own_power, 0)
+
+    def weighted(d, carry):
         for p in range(EXT):
-            wr[p] = wt[p] * zr[i, p]
-            wi[p] = wt[p] * zi[i, p]
-
-        def second_date(j, carry):
+            wr[d, p] = wt[p] * zr[d, p]
+            wi[d, p] = wt[p] * zi[d, p]
+        return carry
+
+    lax.fori_loop(0, DATES, weighted, 0)
+
+    def matching(turn, carry):
+        for t in range(DATES // 2):
+            first = lax.rem(turn + t, DATES - 1)
+            second = lax.rem(turn + (DATES - 1 - t), DATES - 1) if t else DATES - 1
+            i, j = jnp.minimum(first, second), jnp.maximum(first, second)
             real, imag = [], []
             for p in range(EXT):
-                a, b, c, d = wr[p], wi[p], zr[j, p], zi[j, p]
+                a, b, c, d = wr[i, p], wi[i, p], zr[j, p], zi[j, p]
                 real.append(a * c + b * d)
                 imag.append(b * c - a * d)
-            real, imag = row_sums(real), row_sums(imag)
+            sums = columns(row_sums(real) + row_sums(imag), t)
             for r in range(FOLD):
                 scale = inv[i, r] * inv[j, r]
-                x = columns(real[r]) * scale
-                y = columns(imag[r]) * scale
+                x = sums[r] * scale
+                y = sums[FOLD + r] * scale
                 R[r, i * DATES + j] = x
                 I[r, i * DATES + j] = y
                 S[r, i * DATES + j] = x + y
                 S[r, j * DATES + i] = x - y
-            return carry
-
-        return lax.fori_loop(i + 1, DATES, second_date, carry)
-
-    lax.fori_loop(0, DATES - 1, first_date, 0)
+        return carry
+
+    lax.fori_loop(0, DATES - 1, matching, 0)
 
     n = iterations[0]
     odd = (n & 1) == 1
@@ -431,8 +471,8 @@
     return pl.BlockSpec(memory_space=pltpu.SMEM)
 
 
-def anywhere():
-    return pl.BlockSpec(memory_space=pl.ANY)
+def hbm():
+    return pl.BlockSpec(memory_space=pltpu.HBM)
 
 
 def shape(*dims):
@@ -454,7 +494,7 @@
     zr, zi, wt = pl.pallas_call(
         halo_kernel,
         out_shape=[shape(DATES, EXT, 8, 128), shape(DATES, EXT, 8, 128), shape(EXT, 8, 128)],
-        in_specs=[anywhere()] * 3,
+        in_specs=[hbm()] * 3,
         out_specs=[vmem()] * 3,
         scratch_shapes=[
             scratch(DATES, EXT, 8, 128),
@@ -475,8 +515,8 @@
         in_specs=[smem(), smem(), vmem(), vmem(), vmem()],
         out_specs=[vmem(), vmem()],
         scratch_shapes=[
-            scratch(EXT, 8, 128),
-            scratch(EXT, 8, 128),
+            scratch(DATES, EXT, 8, 128),
+            scratch(DATES, EXT, 8, 128),
             scratch(DATES, FOLD, 8, 128),
             scratch(FOLD, DATES * DATES, 8, 128),
             scratch(FOLD, DATES * DATES, 8, 128),
@@ -486,6 +526,8 @@
             scratch(DATES * DATES, 8, 128),
             scratch(DATES, 8, 128),
             scratch(2 * DATES, 8, 128),
+            pltpu.VMEM((256, 256), jnp.bfloat16),
+            scratch(DATES // 2, 16 * FOLD + 16, 128),
         ],
         compiler_params=pltpu.CompilerParams(vmem_limit_bytes=40 << 20),
         name="power",

time: 70.7 us -> 62.9 us (0.89)
  the two profiles are of different devices: /device:TPU:64 before, /device:TPU:8 now
where the time goes in v2:
time: 62.9 us; the launch traced here: 62.7 us
  Pallas kernels  57.3 us (91%)
  local copies, waits for them, and re-layouts  2.86 us (5%)
  between operations  1.35 us (2%)
  other arithmetic  1.15 us (2%)
    pallas_call x1, Pallas kernels, local(): pl.pallas_call(link_kernel, out_shape=shape(2, 4 * ROWS, 128), in_specs=[...  29.8 us
    pallas_call x1, Pallas kernels, local(): pl.pallas_call(main_kernel, out_shape=[shape(2 * DATES, 4 * ROWS, 128), s...  18.1 us
    pallas_call x1, Pallas kernels, local(): pl.pallas_call(halo_kernel, out_shape=[shape(DATES, EXT, 8, 128), shape(D...  9.36 us
    unnamed x6, local copies, waits for them, and re-layouts  2.85 us

profile of v2, /device:TPU:8, one launch (start us, length us, event | category | flops | bytes accessed | tf_op | source)
XLA Modules:
  0.0 62.7 jit_solution(11212298580024932378)
XLA Ops:
  1.3 0.0 copy-start
  1.3 1.0 %copy-done = f32[10,24,512]{2,1,0:T(8,128)S(1)} copy-done((f32[10,24,512]{2,1,0:T(8,128)S(1)}, f32[10,24,512]{2,1,0:T(8,128)}, u32[]{:S(2)}) %copy-start) | copy-done | bytes 491544
  2.3 0.0 copy-start.1
  2.3 1.0 %copy-done.1 = f32[10,24,512]{2,1,0:T(8,128)S(1)} copy-done((f32[10,24,512]{2,1,0:T(8,128)S(1)}, f32[10,24,512]{2,1,0:T(8,128)}, u32[]{:S(2)}) %copy-start.1) | copy-done | bytes 491544
  3.4 0.0 copy-start.2
  3.4 0.8 %copy-done.2 = s32[24,512]{1,0:T(8,128)S(1)} copy-done((s32[24,512]{1,0:T(8,128)S(1)}, s32[24,512]{1,0:T(8,128)}, u32[]{:S(2)}) %copy-start.2) | copy-done | bytes 49176
  4.2 9.4 %halo.1 = (f32[10,22,8,128]{3,2,1,0:T(8,128)S(1)}, f32[10,22,8,128]{3,2,1,0:T(8,128)S(1)}, f32[22,8,128]{2,1,0:T(8,128)S(1)}) custom-call(f32[10,3,4,8,128]{4,3,2,1,0:T(8,128)S(1)} %bitcast.19, f32[10,3,4,8,128]{4,3,2,1,0:T(8,128)S(1)} %bitcast.20, s32[3,4,8,128]{3,2,1,0:T(8,128)S(1)} %bitcast.21), custom_call_target="tpu_custom_call" | custom-call | tf_op jit(solution)/shard_map/halo/pallas_call | solution.py:494
  13.5 18.1 %power.1 = (f32[20,96,128]{2,1,0:T(8,128)S(1)}, f32[2,12,8,128]{3,2,1,0:T(8,128)S(1)}) custom-call(s32[1]{0:T(128)S(6)} %copy.6.iterations, s32[1]{0:T(128)S(6)} %copy.7.chosen, f32[10,22,8,128]{3,2,1,0:T(8,128)S(1)} %get-tuple-element.10.zr, f32[10,22,8,128]{3,2,1,0:T(8,128)S(1)} %get-tuple-element.11.zi, f32[22,8,128]{2,1,0:T(8,128)S(1)} %get-tuple-element.12.wt), custom_call_target="tpu_custom_call" | custom-call | tf_op jit(solution)/shard_map/power/pallas_call | solution.py:512
  31.6 29.8 %links.1 = f32[2,96,128]{2,1,0:T(8,128)S(1)} custom-call(f32[2,12,8,128]{3,2,1,0:T(8,128)S(1)} %get-tuple-element.14.comp, f32[22,8,128]{2,1,0:T(8,128)S(1)} %get-tuple-element.12.wt), custom_call_target="tpu_custom_call" | custom-call | tf_op jit(solution)/shard_map/links/pallas_call | solution.py:535
  61.5 0.1 multiply_subtract_fusion
  61.7 1.0 %maximum_bitcast_fusion = f32[2,10,24,512]{3,2,1,0:T(8,128)} fusion(f32[1,10,3,4,8,128]{5,4,3,2,1,0:T(8,128)S(1)} %bitcast.23, f32[1,10,3,4,8,128]{5,4,3,2,1,0:T(8,128)S(1)} %bitcast.22), kind=kLoop, calls=%fused_computation | loop fusion | flops 245760 | bytes 1966080 | tf_op jit(solution)/shard_map/reshape | solution.py:563
  (1 shorter events, 0.0 us)
Async XLA Ops:
  1.3 1.0 %copy-start = (f32[10,24,512]{2,1,0:T(8,128)S(1)}, f32[10,24,512]{2,1,0:T(8,128)}, u32[]{:S(2)}) copy-start(f32[10,24,512]{2,1,0:T(8,128)} %param.5) | copy-start | bytes 1474564
  2.3 1.0 %copy-start.1 = (f32[10,24,512]{2,1,0:T(8,128)S(1)}, f32[10,24,512]{2,1,0:T(8,128)}, u32[]{:S(2)}) copy-start(f32[10,24,512]{2,1,0:T(8,128)} %param.6) | copy-start | bytes 1474564
  3.4 0.8 %copy-start.2 = (s32[24,512]{1,0:T(8,128)S(1)}, s32[24,512]{1,0:T(8,128)}, u32[]{:S(2)}) copy-start(s32[24,512]{1,0:T(8,128)} %param.7) | copy-start | bytes 147460

commit v3 on v2

--- a/solution.py
+++ b/solution.py
@@ -14,6 +14,10 @@
 TILES = ROWS // 8
 MASKED = 0.125
 FLOOR = 0.03
+LEAST_TURNS = (10 - 1) // 2
+MOST_TURNS = (20 - 1) // 2
+THIRD = 40
+STAGES = ((4, ((0, 5), (19, 5))), (8, ((5, 4), (15, 4))), (11, ((9, 6),)))
 F32 = jnp.float32
 
 SIN = (1.0, -1.0 / 6, 1.0 / 120, -1.0 / 5040, 1.0 / 362880, -1.0 / 39916800)
@@ -44,20 +48,24 @@
     return lax.broadcasted_iota(jnp.int32, (8, 128), 1)
 
 
-def column_sum():
+def column_windows():
     lane, block = lanes(), sublanes() & 3
     not_first = jnp.where(block > 0, 1.0, 0.0).astype(F32)
     not_last = jnp.where(block < 3, 1.0, 0.0).astype(F32)
-    edges = [(amount, lane >= 128 - amount, lane < amount) for amount in (1, 2)]
-
-    def apply(x):
-        before = pltpu.roll(x, 1, 0) * not_first
-        after = pltpu.roll(x, 7, 0) * not_last
-        total = x
-        for amount, high, low in edges:
-            total = total + pltpu.roll(jnp.where(high, before, x), amount, 1)
-            total = total + pltpu.roll(jnp.where(low, after, x), 128 - amount, 1)
-        return total
+
+    def apply(x, y):
+        out = []
+        for q in range(4):
+            pair = (x, y)
+            if q == 0:
+                pair = [jnp.where(lane >= 126, pltpu.roll(v, 1, 0) * not_first, v) for v in pair]
+            if q == 3:
+                pair = [jnp.where(lane < 2, pltpu.roll(v, 7, 0) * not_last, v) for v in pair]
+            first, second = pair
+            start = 2 - 32 * q
+            window = jnp.where(lane < THIRD, pltpu.roll(first, start % 128, 1), pltpu.roll(second, (start + THIRD) % 128, 1))
+            out.append(jnp.where(lane < 2 * THIRD, window, pltpu.roll(first, (start + 2 * THIRD) % 128, 1)))
+        return out
 
     return apply
 
@@ -108,6 +116,18 @@
     return out
 
 
+def long_row_sums(values):
+    count = len(values)
+    heads, tails = list(values), list(values)
+    for p in range(count):
+        if p % 11:
+            heads[p] = heads[p - 1] + values[p]
+    for p in range(count - 2, -1, -1):
+        if p % 11 != 10:
+            tails[p] = tails[p + 1] + values[p]
+    return [tails[r] if r % 11 == 0 else tails[r] + heads[r + 10] for r in range(count - 10)]
+
+
 def halo_kernel(amp, pha, val, zr, zi, wt, A, B, V, local, send, recv):
     count = lax.axis_size("space")
     me = lax.axis_index("space")
@@ -177,7 +197,27 @@
         wt[p] = jnp.where(V[p] == 1, 1.0, MASKED).astype(F32) * inside
 
 
-def main_kernel(iterations, chosen, zr, zi, wt, linked, comp, wr, wi, inv, R, I, S, QR, QI, QS, QD, vec, band, spill):
+def main_kernel(
+    iterations, chosen, zr, zi, wt, linked, datum,
+    wr, wi, inv, R, I, S, QR, QI, QS, QD, vec, band, spill,
+    cut, weight, strips, links, parts, whole, send, recv, own, back_send, back_recv,
+):
+    stacks, spaces = lax.axis_size("tm"), lax.axis_size("space")
+    m, s = lax.axis_index("tm"), lax.axis_index("space")
+    up, down = lax.rem(s + spaces - 1, spaces), lax.rem(s + 1, spaces)
+    barrier = pltpu.get_barrier_semaphore()
+
+    def greet(k, carry):
+        for space in (up, s, down):
+
+            @pl.when((k != m) | (space != s))
+            def _():
+                pl.semaphore_signal(barrier, inc=1, device_id={"tm": k, "space": space}, device_id_type=MESH)
+
+        return carry
+
+    lax.fori_loop(0, stacks, greet, 0)
+
     band[...] = band_matrix()
     columns = column_sums(band, spill)
 
@@ -221,6 +261,14 @@
         return carry
 
     lax.fori_loop(0, DATES - 1, matching, 0)
+
+    windows = column_windows()
+    for p in range(REACH + FOLD):
+        for q, window in enumerate(windows(wt[p], wt[p])):
+            weight[p, 4 * q : 4 * q + 4] = window[:4]
+            weight[ROWS + 2 * REACH - 1 - p, 4 * q : 4 * q + 4] = window[4:]
+
+    pl.semaphore_wait(barrier, 3 * stacks - 1)
 
     n = iterations[0]
     odd = (n & 1) == 1
@@ -289,7 +337,7 @@
         two_r, two_i = row_total(lambda k: QR[k], lambda k: QI[k], lambda i: QD[i])
         start = [jnp.where(odd, a, b) for a, b in zip(one_r + one_i, two_r + two_i)]
 
-        def turn(_, v):
+        def turn(count, v):
             vr, vi = v[:DATES], v[DATES:]
             both = [a + b for a, b in zip(vr, vi)]
             out_r, out_i = [], []
@@ -312,7 +360,11 @@
                 out_i.append(d * vi[i] + (mixed - (rr + ii)))
             return out_r + out_i
 
-        v = lax.fori_loop(0, turns, turn, start)
+        def maybe(count, v):
+            return [jnp.where(count < turns, a, b) for a, b in zip(turn(count, v), v)]
+
+        v = lax.fori_loop(0, LEAST_TURNS, turn, start)
+        v = lax.fori_loop(LEAST_TURNS, MOST_TURNS, maybe, v)
         total = None
         for x in v:
             total = x * x if total is None else total + x * x
@@ -328,8 +380,9 @@
             y = vr[t] * b - vi[t] * a
             cr = x if cr is None else cr + x
             ci = y if ci is None else ci + y
-        comp[0, r] = cr
-        comp[1, r] = ci
+        for q, window in enumerate(windows(cr, ci)):
+            cut[r, 4 * q : 4 * q + 4] = window[:4]
+            cut[ROWS - 1 - r, 4 * q : 4 * q + 4] = window[4:]
         ref_r, ref_i = DATES * vec[ref], DATES * vec[DATES + ref]
         for t in range(DATES):
             x = vr[t] * ref_r + vi[t] * ref_i
@@ -338,129 +391,118 @@
                 for half, row in ((0, r), (1, ROWS - 1 - r)):
                     first = (row >> 3) * 32 + (row & 7)
                     linked[part, pl.ds(first, 4, stride=8), :] = value[4 * half : 4 * half + 4]
+        for last, pieces in STAGES:
+
+            @pl.when(r == last)
+            def _():
+                lax.fori_loop(0, stacks, lambda k, c: share(k, c, pieces), 0)
+
         return carry
 
-    lax.fori_loop(0, FOLD, position, 0)
-
-
-def link_kernel(comp, wt, datum, near, own_edge, near_edge, u, got, ready, dat, sem, send_u, recv_u, send_d, recv_d):
-    stacks, spaces = lax.axis_size("tm"), lax.axis_size("space")
-    m, s = lax.axis_index("tm"), lax.axis_index("space")
-    before, after = lax.rem(m + stacks - 1, stacks), lax.rem(m + 1, stacks)
-    up, down = lax.rem(s + spaces - 1, spaces), lax.rem(s + 1, spaces)
-
-    barrier = pltpu.get_barrier_semaphore()
-
-    def greet(tm, space):
-        pl.semaphore_signal(barrier, inc=1, device_id={"tm": tm, "space": space}, device_id_type=MESH)
-
-    for step in range(1, stacks):
-        greet(lax.rem(m + step, stacks), s)
-    for space in (up, down):
-        greet(m, space)
-        greet(before, space)
-        greet(after, space)
-    pl.semaphore_wait(barrier, stacks - 1 + 6)
-
-    heads, tails = pl.ds(0, 4), pl.ds(4, 4)
-    edge = pl.ds(0, REACH)
-    plan = (
-        (comp, near, (before, s)),
-        (comp.at[:, edge, tails], own_edge.at[:, :, heads], (m, down)),
-        (comp.at[:, edge, heads], own_edge.at[:, :, tails], (m, up)),
-        (comp.at[:, edge, tails], near_edge.at[:, :, heads], (before, down)),
-        (comp.at[:, edge, heads], near_edge.at[:, :, tails], (before, up)),
-    )
-    copies = []
-    for k, (source, target, (tm, space)) in enumerate(plan):
-        copy = pltpu.make_async_remote_copy(
-            source, target, sem.at[0, k], sem.at[1, k], device_id={"tm": tm, "space": space}, device_id_type=MESH
-        )
-        copy.start()
-        copies.append(copy)
-    for copy in copies:
-        copy.wait()
-
-    def extended(block, edges, part):
-        rows = [edges[part, REACH - 1 - k] for k in range(REACH)]
-        rows += [block[part, r] for r in range(FOLD)]
-        rows += [pltpu.roll(block[part, FOLD - 1 - k], 4, 0) for k in range(REACH)]
-        return rows
-
-    ar, ai = extended(comp, own_edge, 0), extended(comp, own_edge, 1)
-    br, bi = extended(near, near_edge, 0), extended(near, near_edge, 1)
-    columns = column_sum()
-    cross_r, cross_i, power_a, power_b = [], [], [], []
-    for p in range(EXT):
-        w = wt[p]
-        xr, xi = w * ar[p], w * ai[p]
-        cross_r.append(xr * br[p] + xi * bi[p])
-        cross_i.append(xi * br[p] - xr * bi[p])
-        power_a.append(xr * ar[p] + xi * ai[p])
-        power_b.append(w * (br[p] * br[p] + bi[p] * bi[p]))
-    cross_r, cross_i, power_a, power_b = [row_sums(x) for x in (cross_r, cross_i, power_a, power_b)]
-    for r in range(FOLD):
-        scale = lax.rsqrt((columns(power_a[r]) + 1.0) * (columns(power_b[r]) + 1.0))
-        x, y = columns(cross_r[r]) * scale, columns(cross_i[r]) * scale
-        bounded = lax.rsqrt(jnp.maximum(x * x + y * y, FLOOR * FLOOR))
-        u[r, 0] = x * bounded
-        u[r, 1] = y * bounded
-
-    def u_copy(step):
-        to = lax.rem(m + step, stacks)
-        return to, pltpu.make_async_remote_copy(
-            u.at[to], got.at[m], send_u.at[to], recv_u.at[m], device_id={"tm": to}, device_id_type=MESH
-        )
-
-    for step in range(1, stacks):
-        to = lax.rem(m + step, stacks)
-
-        @pl.when(to < FOLD)
-        def _():
-            u_copy(step)[1].start()
-
-    @pl.when(m < FOLD)
-    def _():
-        got[m] = u[m]
-        xr, xi = jnp.ones((8, 128), F32), jnp.zeros((8, 128), F32)
-        for k in range(stacks):
-            ready[k, 0] = xr
-            ready[k, 1] = xi
+    def share(k, carry, pieces):
+        def start(first, size, to, space):
+            pltpu.make_async_remote_copy(
+                cut.at[pl.ds(first, size), k],
+                strips.at[pl.ds(to, size), m],
+                send,
+                recv,
+                device_id={"tm": k, "space": space},
+                device_id_type=MESH,
+            ).start()
+
+        for first, size in pieces:
 
             @pl.when(k != m)
             def _():
-                pltpu.make_async_remote_copy(
-                    ready.at[k], dat.at[m], send_d.at[k], recv_d.at[m], device_id={"tm": k}, device_id_type=MESH
-                ).start()
-
-            @pl.when(k != m)
-            def _():
-                pltpu.make_async_copy(got.at[k], got.at[k], recv_u.at[k]).wait()
-
-            lr, li = got[k, 0], got[k, 1]
-            xr, xi = xr * lr - xi * li, xr * li + xi * lr
-        dat[m] = ready[m]
-
-    for r in range(FOLD):
-
-        @pl.when(r != m)
+                start(first, size, REACH + first, s)
+
+            if first == 0:
+                start(first, REACH, REACH + ROWS, up)
+            if first + size == ROWS:
+                start(first + size - REACH, REACH, 0, down)
+        return carry
+
+    lax.fori_loop(0, FOLD, position, 0)
+
+    mine = pltpu.make_async_copy(cut.at[:, m], strips.at[pl.ds(REACH, ROWS), m], own)
+    mine.start()
+    mine.wait()
+    everything = strips.at[:, pl.ds(0, 13)]
+    pltpu.make_async_copy(everything, everything, recv).wait()
+    lane, sub = lanes(), sublanes()
+    halves = (pl.ds(0, 8), pl.ds(8, 8))
+
+    def next_stack(pair):
+        second = pltpu.roll(pair[1], 7, 0)
+        return jnp.where(sub < 7, pltpu.roll(pair[0], 7, 0), second), second
+
+    low, middle = lane < THIRD, lane < 2 * THIRD
+    fields = ([], [])
+    for p in range(ROWS + 2 * REACH):
+        w = jnp.broadcast_to(weight[p, pl.ds(m, 1)], (8, 128))
+        pair = [strips[p, half] for half in halves]
+        for field, x, y in zip(fields, pair, next_stack(pair)):
+            straight = x * y
+            crossed = x * pltpu.roll(y, 128 - THIRD, 1)
+            power = x * x
+            value = jnp.where(
+                low,
+                straight + pltpu.roll(straight, 128 - THIRD, 1),
+                jnp.where(
+                    middle, crossed - pltpu.roll(crossed, THIRD, 1), power + pltpu.roll(power, THIRD, 1)
+                ),
+            )
+            field.append(w * value)
+    sums = [long_row_sums(field) for field in fields]
+    for r in range(ROWS):
+        pair = []
+        for half in range(2):
+            x = sums[half][r]
+            for amount in (1, 2, 127, 126):
+                x = x + pltpu.roll(sums[half][r], amount, 1)
+            pair.append(x)
+        for half, x, y in zip(halves, pair, next_stack(pair)):
+            scale = lax.rsqrt((x + 1.0) * (y + 1.0))
+            x = x * jnp.where(low, pltpu.roll(scale, 128 - 2 * THIRD, 1), pltpu.roll(scale, 128 - THIRD, 1))
+            size = x * x
+            size = size + jnp.where(low, pltpu.roll(size, 128 - THIRD, 1), pltpu.roll(size, THIRD, 1))
+            first = 16 * r + (half.start)
+            links[pl.ds(first, 8)] = x * lax.rsqrt(jnp.maximum(size, FLOOR * FLOOR))
+
+    xr = [jnp.ones((8, 128), F32)] * TILES
+    xi = [jnp.zeros((8, 128), F32)] * TILES
+    for k in range(stacks):
+        for t in range(TILES):
+            parts[k, 8 * t : 8 * t + 8] = jnp.where(low, xr[t], pltpu.roll(xi[t], THIRD, 1))
+
+        @pl.when(k != m)
         def _():
-            pltpu.make_async_copy(dat.at[r], dat.at[r], recv_d.at[r]).wait()
-            pltpu.make_async_copy(u.at[r], u.at[r], send_u.at[r]).wait()
-
-    for r in range(FOLD):
-        for part in range(2):
-            value = dat[r, part]
-            for half, row in ((0, r), (1, ROWS - 1 - r)):
-                datum[part, pl.ds((row // 8) * 32 + row % 8, 4, stride=8), :] = value[4 * half : 4 * half + 4]
-
-    @pl.when(m < FOLD)
-    def _():
-        for k in range(stacks):
-
-            @pl.when(k != m)
-            def _():
-                pltpu.make_async_copy(ready.at[k], ready.at[k], send_d.at[k]).wait()
+            pltpu.make_async_remote_copy(
+                parts.at[k], whole.at[m], back_send, back_recv, device_id={"tm": k}, device_id_type=MESH
+            ).start()
+
+        if k < stacks - 1:
+            for t in range(TILES):
+                lr = links[pl.ds(128 * t + k, 8, stride=16)]
+                li = pltpu.roll(lr, 128 - THIRD, 1)
+                xr[t], xi[t] = xr[t] * lr - xi[t] * li, xr[t] * li + xi[t] * lr
+    whole[m] = parts[m]
+    most = whole.at[pl.ds(0, stacks - 1)]
+    pltpu.make_async_copy(most, most, back_recv).wait()
+
+    for t in range(TILES):
+        for b in range(4):
+            real, imag = None, None
+            for q in range(4):
+                x = whole[4 * q + b, 8 * t : 8 * t + 8]
+                a = pltpu.roll(x, (32 * q - 2) % 128, 1)
+                c = pltpu.roll(x, (32 * q - 2 - THIRD) % 128, 1)
+                real = a if q == 0 else jnp.where(lane < 32 * q, real, a)
+                imag = c if q == 0 else jnp.where(lane < 32 * q, imag, c)
+            datum[0, 8 * (4 * t + b) : 8 * (4 * t + b) + 8] = real
+            datum[1, 8 * (4 * t + b) : 8 * (4 * t + b) + 8] = imag
+    pltpu.make_async_copy(everything, everything, send).wait()
+    pltpu.make_async_copy(most, most, back_send).wait()
 
 
 def vmem():
@@ -509,9 +551,9 @@
         ),
         name="halo",
     )(tiled(amplitude), tiled(phase), tiled(validity))
-    linked, comp = pl.pallas_call(
+    linked, datum = pl.pallas_call(
         main_kernel,
-        out_shape=[shape(2 * DATES, 4 * ROWS, 128), shape(2, FOLD, 8, 128)],
+        out_shape=[shape(2 * DATES, 4 * ROWS, 128), shape(2, 4 * ROWS, 128)],
         in_specs=[smem(), smem(), vmem(), vmem(), vmem()],
         out_specs=[vmem(), vmem()],
         scratch_shapes=[
@@ -528,34 +570,23 @@
             scratch(2 * DATES, 8, 128),
             pltpu.VMEM((256, 256), jnp.bfloat16),
             scratch(DATES // 2, 16 * FOLD + 16, 128),
+            scratch(ROWS, 16, 128),
+            scratch(ROWS + 2 * REACH, 16, 128),
+            scratch(40, 16, 128),
+            scratch(16 * ROWS, 128),
+            scratch(16, ROWS, 128),
+            scratch(16, ROWS, 128),
+            dma(()),
+            dma(()),
+            dma(()),
+            dma(()),
+            dma(()),
         ],
-        compiler_params=pltpu.CompilerParams(vmem_limit_bytes=40 << 20),
+        compiler_params=pltpu.CompilerParams(
+            collective_id=1, has_side_effects=True, vmem_limit_bytes=40 << 20
+        ),
         name="power",
     )(iterations, reference_date, zr, zi, wt)
-    datum = pl.pallas_call(
-        link_kernel,
-        out_shape=shape(2, 4 * ROWS, 128),
-        in_specs=[vmem(), vmem()],
-        out_specs=vmem(),
-        scratch_shapes=[
-            scratch(2, FOLD, 8, 128),
-            scratch(2, REACH, 8, 128),
-            scratch(2, REACH, 8, 128),
-            scratch(16, 2, 8, 128),
-            scratch(16, 2, 8, 128),
-            scratch(16, 2, 8, 128),
-            scratch(16, 2, 8, 128),
-            dma((2, 5)),
-            dma((16,)),
-            dma((16,)),
-            dma((16,)),
-            dma((16,)),
-        ],
-        compiler_params=pltpu.CompilerParams(
-            collective_id=1, has_side_effects=True, vmem_limit_bytes=16 << 20
-        ),
-        name="links",
-    )(comp, wt)
     lr, li = linked[:DATES], linked[DATES:]
     dr, di = datum[0], datum[1]
     out = jnp.stack([lr * dr - li * di, lr * di + li * dr])

time: 62.9 us -> 55.8 us (0.89)
  the two profiles are of different devices: /device:TPU:8 before, /device:TPU:7 now
where the time goes in v3:
time: 55.8 us; the launch traced here: 55.5 us
  Pallas kernels  50.2 us (90%)
  local copies, waits for them, and re-layouts  2.86 us (5%)
  between operations  1.34 us (2%)
  other arithmetic  1.15 us (2%)
    pallas_call x1, Pallas kernels, local(): pl.pallas_call(main_kernel, out_shape=[shape(2 * DATES, 4 * ROWS, 128), s...  41.2 us
    pallas_call x1, Pallas kernels, local(): pl.pallas_call(halo_kernel, out_shape=[shape(DATES, EXT, 8, 128), shape(D...  8.98 us
    unnamed x6, local copies, waits for them, and re-layouts  2.85 us

profile of v3, /device:TPU:7, one launch (start us, length us, event | category | flops | bytes accessed | tf_op | source)
XLA Modules:
  0.0 55.5 jit_solution(7917176414211008036)
XLA Ops:
  1.3 0.0 copy-start
  1.3 1.0 %copy-done = f32[10,24,512]{2,1,0:T(8,128)S(1)} copy-done((f32[10,24,512]{2,1,0:T(8,128)S(1)}, f32[10,24,512]{2,1,0:T(8,128)}, u32[]{:S(2)}) %copy-start) | copy-done | bytes 491544
  2.3 0.0 copy-start.1
  2.3 1.0 %copy-done.1 = f32[10,24,512]{2,1,0:T(8,128)S(1)} copy-done((f32[10,24,512]{2,1,0:T(8,128)S(1)}, f32[10,24,512]{2,1,0:T(8,128)}, u32[]{:S(2)}) %copy-start.1) | copy-done | bytes 491544
  3.4 0.0 copy-start.2
  3.4 0.8 %copy-done.2 = s32[24,512]{1,0:T(8,128)S(1)} copy-done((s32[24,512]{1,0:T(8,128)S(1)}, s32[24,512]{1,0:T(8,128)}, u32[]{:S(2)}) %copy-start.2) | copy-done | bytes 49176
  4.2 9.0 %halo.1 = (f32[10,22,8,128]{3,2,1,0:T(8,128)S(1)}, f32[10,22,8,128]{3,2,1,0:T(8,128)S(1)}, f32[22,8,128]{2,1,0:T(8,128)S(1)}) custom-call(f32[10,3,4,8,128]{4,3,2,1,0:T(8,128)S(1)} %bitcast.19, f32[10,3,4,8,128]{4,3,2,1,0:T(8,128)S(1)} %bitcast.20, s32[3,4,8,128]{3,2,1,0:T(8,128)S(1)} %bitcast.21), custom_call_target="tpu_custom_call" | custom-call | tf_op jit(solution)/shard_map/halo/pallas_call | solution.py:536
  13.1 41.2 %power.1 = (f32[20,96,128]{2,1,0:T(8,128)S(1)}, f32[2,96,128]{2,1,0:T(8,128)S(1)}) custom-call(s32[1]{0:T(128)S(6)} %copy.6.iterations, s32[1]{0:T(128)S(6)} %copy.7.chosen, f32[10,22,8,128]{3,2,1,0:T(8,128)S(1)} %get-tuple-element.10.zr, f32[10,22,8,128]{3,2,1,0:T(8,128)S(1)} %get-tuple-element.11.zi, f32[22,8,128]{2,1,0:T(8,128)S(1)} %get-tuple-element.12.wt), custom_call_target="tpu_custom_call" | custom-call | tf_op jit(solution)/shard_map/power/pallas_call | solution.py:554
  54.4 0.1 multiply_subtract_fusion
  54.5 1.0 %maximum_bitcast_fusion = f32[2,10,24,512]{3,2,1,0:T(8,128)} fusion(f32[1,10,3,4,8,128]{5,4,3,2,1,0:T(8,128)S(1)} %bitcast.23, f32[1,10,3,4,8,128]{5,4,3,2,1,0:T(8,128)S(1)} %bitcast.22), kind=kLoop, calls=%fused_computation | loop fusion | flops 245760 | bytes 1966080 | tf_op jit(solution)/shard_map/reshape | solution.py:594
  (1 shorter events, 0.0 us)
Async XLA Ops:
  1.3 1.0 %copy-start = (f32[10,24,512]{2,1,0:T(8,128)S(1)}, f32[10,24,512]{2,1,0:T(8,128)}, u32[]{:S(2)}) copy-start(f32[10,24,512]{2,1,0:T(8,128)} %param.5) | copy-start | bytes 1474564
  2.3 1.0 %copy-start.1 = (f32[10,24,512]{2,1,0:T(8,128)S(1)}, f32[10,24,512]{2,1,0:T(8,128)}, u32[]{:S(2)}) copy-start(f32[10,24,512]{2,1,0:T(8,128)} %param.6) | copy-start | bytes 1474564
  3.4 0.8 %copy-start.2 = (s32[24,512]{1,0:T(8,128)S(1)}, s32[24,512]{1,0:T(8,128)}, u32[]{:S(2)}) copy-start(s32[24,512]{1,0:T(8,128)} %param.7) | copy-start | bytes 147460

commit v4 on v3

--- a/solution.py
+++ b/solution.py
@@ -137,6 +137,9 @@
     def lead(source):
         return (slice(None),) * (len(source.shape) - 4)
 
+    barrier = pltpu.get_barrier_semaphore()
+    for neighbour in (up, down):
+        pl.semaphore_signal(barrier, inc=1, device_id={"space": neighbour}, device_id_type=MESH)
     for k, (source, target) in enumerate(arrays):
         all_ = lead(source)
         for r in range(FOLD + REACH):
@@ -147,9 +150,6 @@
                     local.at[k],
                 ).start()
 
-    barrier = pltpu.get_barrier_semaphore()
-    for neighbour in (up, down):
-        pl.semaphore_signal(barrier, inc=1, device_id={"space": neighbour}, device_id_type=MESH)
     pl.semaphore_wait(barrier, 2)
 
     for k, (source, target) in enumerate(arrays):
@@ -198,22 +198,19 @@
 
 
 def main_kernel(
-    iterations, chosen, zr, zi, wt, linked, datum,
+    iterations, chosen, zr, zi, wt, linked_r, linked_i, datum, turned_datum,
     wr, wi, inv, R, I, S, QR, QI, QS, QD, vec, band, spill,
-    cut, weight, strips, links, parts, whole, send, recv, own, back_send, back_recv,
+    cut, weight, far_weight, strips, links, parts, whole, send, recv, own, back_send, back_recv,
 ):
     stacks, spaces = lax.axis_size("tm"), lax.axis_size("space")
     m, s = lax.axis_index("tm"), lax.axis_index("space")
-    up, down = lax.rem(s + spaces - 1, spaces), lax.rem(s + 1, spaces)
+    partner = lax.rem(s + spaces // 2, spaces)
+    up, down = lax.rem(partner + spaces - 1, spaces), lax.rem(partner + 1, spaces)
     barrier = pltpu.get_barrier_semaphore()
 
     def greet(k, carry):
-        for space in (up, s, down):
-
-            @pl.when((k != m) | (space != s))
-            def _():
-                pl.semaphore_signal(barrier, inc=1, device_id={"tm": k, "space": space}, device_id_type=MESH)
-
+        for space in (up, partner, down):
+            pl.semaphore_signal(barrier, inc=1, device_id={"tm": k, "space": space}, device_id_type=MESH)
         return carry
 
     lax.fori_loop(0, stacks, greet, 0)
@@ -268,7 +265,11 @@
             weight[p, 4 * q : 4 * q + 4] = window[:4]
             weight[ROWS + 2 * REACH - 1 - p, 4 * q : 4 * q + 4] = window[4:]
 
-    pl.semaphore_wait(barrier, 3 * stacks - 1)
+    pl.semaphore_wait(barrier, 3 * stacks)
+    weights = pltpu.make_async_remote_copy(
+        weight.at[:, m], far_weight, *own, device_id={"space": partner}, device_id_type=MESH
+    )
+    weights.start()
 
     n = iterations[0]
     odd = (n & 1) == 1
@@ -387,10 +388,10 @@
         for t in range(DATES):
             x = vr[t] * ref_r + vi[t] * ref_i
             y = vi[t] * ref_r - vr[t] * ref_i
-            for part, value in ((t, x), (DATES + t, y)):
+            for target, value in ((linked_r, x), (linked_i, y)):
                 for half, row in ((0, r), (1, ROWS - 1 - r)):
                     first = (row >> 3) * 32 + (row & 7)
-                    linked[part, pl.ds(first, 4, stride=8), :] = value[4 * half : 4 * half + 4]
+                    target[t, pl.ds(first, 4, stride=8), :] = value[4 * half : 4 * half + 4]
         for last, pieces in STAGES:
 
             @pl.when(r == last)
@@ -412,10 +413,7 @@
 
         for first, size in pieces:
 
-            @pl.when(k != m)
-            def _():
-                start(first, size, REACH + first, s)
-
+            start(first, size, REACH + first, partner)
             if first == 0:
                 start(first, REACH, REACH + ROWS, up)
             if first + size == ROWS:
@@ -424,11 +422,8 @@
 
     lax.fori_loop(0, FOLD, position, 0)
 
-    mine = pltpu.make_async_copy(cut.at[:, m], strips.at[pl.ds(REACH, ROWS), m], own)
-    mine.start()
-    mine.wait()
-    everything = strips.at[:, pl.ds(0, 13)]
-    pltpu.make_async_copy(everything, everything, recv).wait()
+    weights.wait()
+    pltpu.make_async_copy(strips, strips, recv).wait()
     lane, sub = lanes(), sublanes()
     halves = (pl.ds(0, 8), pl.ds(8, 8))
 
@@ -436,10 +431,10 @@
         second = pltpu.roll(pair[1], 7, 0)
         return jnp.where(sub < 7, pltpu.roll(pair[0], 7, 0), second), second
 
-    low, middle = lane < THIRD, lane < 2 * THIRD
+    low, middle, left = lane < THIRD, lane < 2 * THIRD, lane < 64
     fields = ([], [])
     for p in range(ROWS + 2 * REACH):
-        w = jnp.broadcast_to(weight[p, pl.ds(m, 1)], (8, 128))
+        w = jnp.broadcast_to(far_weight[pl.ds(p, 1)], (8, 128))
         pair = [strips[p, half] for half in halves]
         for field, x, y in zip(fields, pair, next_stack(pair)):
             straight = x * y
@@ -458,7 +453,7 @@
         pair = []
         for half in range(2):
             x = sums[half][r]
-            for amount in (1, 2, 127, 126):
+            for amount in (127, 126, 125, 124):
                 x = x + pltpu.roll(sums[half][r], amount, 1)
             pair.append(x)
         for half, x, y in zip(halves, pair, next_stack(pair)):
@@ -472,36 +467,42 @@
     xr = [jnp.ones((8, 128), F32)] * TILES
     xi = [jnp.zeros((8, 128), F32)] * TILES
     for k in range(stacks):
-        for t in range(TILES):
-            parts[k, 8 * t : 8 * t + 8] = jnp.where(low, xr[t], pltpu.roll(xi[t], THIRD, 1))
-
-        @pl.when(k != m)
-        def _():
-            pltpu.make_async_remote_copy(
-                parts.at[k], whole.at[m], back_send, back_recv, device_id={"tm": k}, device_id_type=MESH
-            ).start()
-
+        tiles = [jnp.where(lane < 32, xr[t], pltpu.roll(xi[t], 32, 1)) for t in range(TILES)]
+        parts[k, 0:8] = jnp.where(left, tiles[0], pltpu.roll(tiles[1], 64, 1))
+        parts[k, 8:16] = jnp.where(left, tiles[2], pltpu.roll(pltpu.roll(tiles[2], 64, 1), 4, 0))
+        pltpu.make_async_remote_copy(
+            parts.at[k, pl.ds(0, 12)],
+            whole.at[m, pl.ds(0, 12)],
+            back_send,
+            back_recv,
+            device_id={"tm": k, "space": partner},
+            device_id_type=MESH,
+        ).start()
         if k < stacks - 1:
             for t in range(TILES):
                 lr = links[pl.ds(128 * t + k, 8, stride=16)]
                 li = pltpu.roll(lr, 128 - THIRD, 1)
                 xr[t], xi[t] = xr[t] * lr - xi[t] * li, xr[t] * li + xi[t] * lr
-    whole[m] = parts[m]
-    most = whole.at[pl.ds(0, stacks - 1)]
+    most = whole.at[:, pl.ds(0, 12)]
     pltpu.make_async_copy(most, most, back_recv).wait()
 
-    for t in range(TILES):
-        for b in range(4):
-            real, imag = None, None
-            for q in range(4):
-                x = whole[4 * q + b, 8 * t : 8 * t + 8]
-                a = pltpu.roll(x, (32 * q - 2) % 128, 1)
-                c = pltpu.roll(x, (32 * q - 2 - THIRD) % 128, 1)
-                real = a if q == 0 else jnp.where(lane < 32 * q, real, a)
-                imag = c if q == 0 else jnp.where(lane < 32 * q, imag, c)
-            datum[0, 8 * (4 * t + b) : 8 * (4 * t + b) + 8] = real
-            datum[1, 8 * (4 * t + b) : 8 * (4 * t + b) + 8] = imag
-    pltpu.make_async_copy(everything, everything, send).wait()
+    for b in range(4):
+        joined = [None] * 6
+        for q in range(4):
+            x, y = whole[4 * q + b, 0:8], whole[4 * q + b, 8:16]
+            y = jnp.where(sub < 4, y, pltpu.roll(pltpu.roll(y, 64, 1), 4, 0))
+            for n in range(6):
+                source, quarter = (x, n) if n < 4 else (y, n - 4)
+                amount = 32 * (q - quarter) % 128
+                turned = pltpu.roll(source, amount, 1) if amount else source
+                joined[n] = turned if q == 0 else jnp.where(lane < 32 * q, joined[n], turned)
+        for t in range(TILES):
+            rows = pl.ds(8 * (4 * t + b), 8)
+            datum[0, rows] = joined[2 * t]
+            datum[1, rows] = joined[2 * t + 1]
+            turned_datum[0, rows] = -joined[2 * t + 1]
+            turned_datum[1, rows] = joined[2 * t]
+    pltpu.make_async_copy(strips, strips, send).wait()
     pltpu.make_async_copy(most, most, back_send).wait()
 
 
@@ -550,12 +551,12 @@
             collective_id=0, has_side_effects=True, vmem_limit_bytes=16 << 20
         ),
         name="halo",
-    )(tiled(amplitude), tiled(phase), tiled(validity))
-    linked, datum = pl.pallas_call(
+    )(*[pltpu.with_memory_space_constraint(tiled(x), pltpu.HBM) for x in (amplitude, phase, validity)])
+    linked_r, linked_i, datum, turned = pl.pallas_call(
         main_kernel,
-        out_shape=[shape(2 * DATES, 4 * ROWS, 128), shape(2, 4 * ROWS, 128)],
+        out_shape=[shape(DATES, 4 * ROWS, 128)] * 2 + [shape(2, 4 * ROWS, 128)] * 2,
         in_specs=[smem(), smem(), vmem(), vmem(), vmem()],
-        out_specs=[vmem(), vmem()],
+        out_specs=[vmem()] * 4,
         scratch_shapes=[
             scratch(DATES, EXT, 8, 128),
             scratch(DATES, EXT, 8, 128),
@@ -572,13 +573,14 @@
             scratch(DATES // 2, 16 * FOLD + 16, 128),
             scratch(ROWS, 16, 128),
             scratch(ROWS + 2 * REACH, 16, 128),
-            scratch(40, 16, 128),
+            scratch(ROWS + 2 * REACH, 128),
+            scratch(ROWS + 2 * REACH, 16, 128),
             scratch(16 * ROWS, 128),
-            scratch(16, ROWS, 128),
-            scratch(16, ROWS, 128),
+            scratch(16, 16, 128),
+            scratch(16, 16, 128),
             dma(()),
             dma(()),
-            dma(()),
+            [dma(()), dma(())],
             dma(()),
             dma(()),
         ],
@@ -587,9 +589,7 @@
         ),
         name="power",
     )(iterations, reference_date, zr, zi, wt)
-    lr, li = linked[:DATES], linked[DATES:]
-    dr, di = datum[0], datum[1]
-    out = jnp.stack([lr * dr - li * di, lr * di + li * dr])
+    out = linked_r * datum[:, None] + linked_i * turned[:, None]
     out = out.reshape(2, DATES, TILES, 4, 8, 128).transpose(0, 1, 2, 4, 3, 5)
     return out.reshape(2, DATES, ROWS, 512)
 

time: 55.8 us -> 50.4 us (0.903)
  the two profiles are of different devices: /device:TPU:7 before, /device:TPU:8 now
where the time goes in v4:
time: 50.4 us; the launch traced here: 50.3 us
  Pallas kernels  47.8 us (95%)
  between operations  1.31 us (3%)
  other arithmetic  1.09 us (2%)
    pallas_call x1, Pallas kernels, local(): pl.pallas_call(main_kernel, out_shape=[shape(DATES, 4 * ROWS, 128)] * 2 +...  39.2 us
    pallas_call x1, Pallas kernels, local(): pl.pallas_call(halo_kernel, out_shape=[shape(DATES, EXT, 8, 128), shape(D...  8.64 us
    add x1, other arithmetic, local(): out = linked_r * datum[:, None] + linked_i * turned[:, None]  1.09 us

profile of v4, /device:TPU:8, one launch (start us, length us, event | category | flops | bytes accessed | tf_op | source)
XLA Modules:
  0.0 50.3 jit_solution(15324516334030472686)
XLA Ops:
  1.3 8.6 %halo.1 = (f32[10,22,8,128]{3,2,1,0:T(8,128)S(1)}, f32[10,22,8,128]{3,2,1,0:T(8,128)S(1)}, f32[22,8,128]{2,1,0:T(8,128)S(1)}) custom-call(f32[10,3,4,8,128]{4,3,2,1,0:T(8,128)} %bitcast.33, f32[10,3,4,8,128]{4,3,2,1,0:T(8,128)} %bitcast.34, s32[3,4,8,128]{3,2,1,0:T(8,128)} %bitcast.35), custom_call_target="tpu_custom_call" | custom-call | tf_op jit(solution)/shard_map/halo/pallas_call | solution.py:537
  9.9 39.2 %power.1 = (f32[10,96,128]{2,1,0:T(8,128)S(1)}, f32[10,96,128]{2,1,0:T(8,128)S(1)}, f32[2,96,128]{2,1,0:T(8,128)S(1)}, f32[2,96,128]{2,1,0:T(8,128)S(1)}) custom-call(s32[1]{0:T(128)S(6)} %copy.6.iterations, s32[1]{0:T(128)S(6)} %copy.7.chosen, f32[10,22,8,128]{3,2,1,0:T(8,128)S(1)} %get-tuple-element.12.zr, f32[10,22,8,128]{3,2,1,0:T(8,128)S(1)} %get-tuple-element.13.zi, ...), custom_call_target="tpu_custom_call" | custom-call | tf_op jit(solution)/shard_map/power/pallas_call | solution.py:555
  49.2 1.1 %multiply_add_fusion = f32[2,10,24,512]{3,2,1,0:T(8,128)} fusion(f32[2,24,512]{2,1,0:T(8,128)S(1)} %bitcast.32, f32[10,24,512]{2,1,0:T(8,128)S(1)} %bitcast.30, f32[2,24,512]{2,1,0:T(8,128)S(1)} %bitcast.31, f32[10,24,512]{2,1,0:T(8,128)S(1)} %bitcast.29), kind=kLoop, calls=%fused_computation | loop fusion | flops 737280 | bytes 2162688 | tf_op jit(solution)/shard_map/add | solution.py:592

commit v5 on v4

--- a/solution.py
+++ b/solution.py
@@ -17,7 +17,7 @@
 LEAST_TURNS = (10 - 1) // 2
 MOST_TURNS = (20 - 1) // 2
 THIRD = 40
-STAGES = ((4, ((0, 5), (19, 5))), (8, ((5, 4), (15, 4))), (11, ((9, 6),)))
+STAGES = ((4, ()), (8, ((0, 9), (15, 9))), (11, ((9, 6),)))
 F32 = jnp.float32
 
 SIN = (1.0, -1.0 / 6, 1.0 / 120, -1.0 / 5040, 1.0 / 362880, -1.0 / 39916800)
@@ -414,10 +414,9 @@
         for first, size in pieces:
 
             start(first, size, REACH + first, partner)
-            if first == 0:
-                start(first, REACH, REACH + ROWS, up)
-            if first + size == ROWS:
-                start(first + size - REACH, REACH, 0, down)
+        if not pieces:
+            start(0, REACH, REACH + ROWS, up)
+            start(ROWS - REACH, REACH, 0, down)
         return carry
 
     lax.fori_loop(0, FOLD, position, 0)

time: 50.4 us -> 50.3 us (level)
  no operation moved by 1% of the time
where the time goes in v5:
time: 50.3 us; the launch traced here: 50.1 us
  Pallas kernels  47.7 us (95%)
  between operations  1.31 us (3%)
  other arithmetic  1.09 us (2%)
    pallas_call x1, Pallas kernels, local(): pl.pallas_call(main_kernel, out_shape=[shape(DATES, 4 * ROWS, 128)] * 2 +...  39 us
    pallas_call x1, Pallas kernels, local(): pl.pallas_call(halo_kernel, out_shape=[shape(DATES, EXT, 8, 128), shape(D...  8.64 us
    add x1, other arithmetic, local(): out = linked_r * datum[:, None] + linked_i * turned[:, None]  1.09 us

profile of v5, /device:TPU:8, one launch (start us, length us, event | category | flops | bytes accessed | tf_op | source)
XLA Modules:
  0.0 50.1 jit_solution(4892609361686070277)
XLA Ops:
  1.3 8.6 %halo.1 = (f32[10,22,8,128]{3,2,1,0:T(8,128)S(1)}, f32[10,22,8,128]{3,2,1,0:T(8,128)S(1)}, f32[22,8,128]{2,1,0:T(8,128)S(1)}) custom-call(f32[10,3,4,8,128]{4,3,2,1,0:T(8,128)} %bitcast.33, f32[10,3,4,8,128]{4,3,2,1,0:T(8,128)} %bitcast.34, s32[3,4,8,128]{3,2,1,0:T(8,128)} %bitcast.35), custom_call_target="tpu_custom_call" | custom-call | tf_op jit(solution)/shard_map/halo/pallas_call | solution.py:536
  9.9 39.0 %power.1 = (f32[10,96,128]{2,1,0:T(8,128)S(1)}, f32[10,96,128]{2,1,0:T(8,128)S(1)}, f32[2,96,128]{2,1,0:T(8,128)S(1)}, f32[2,96,128]{2,1,0:T(8,128)S(1)}) custom-call(s32[1]{0:T(128)S(6)} %copy.6.iterations, s32[1]{0:T(128)S(6)} %copy.7.chosen, f32[10,22,8,128]{3,2,1,0:T(8,128)S(1)} %get-tuple-element.12.zr, f32[10,22,8,128]{3,2,1,0:T(8,128)S(1)} %get-tuple-element.13.zi, ...), custom_call_target="tpu_custom_call" | custom-call | tf_op jit(solution)/shard_map/power/pallas_call | solution.py:554
  49.0 1.1 %multiply_add_fusion = f32[2,10,24,512]{3,2,1,0:T(8,128)} fusion(f32[2,24,512]{2,1,0:T(8,128)S(1)} %bitcast.32, f32[10,24,512]{2,1,0:T(8,128)S(1)} %bitcast.30, f32[2,24,512]{2,1,0:T(8,128)S(1)} %bitcast.31, f32[10,24,512]{2,1,0:T(8,128)S(1)} %bitcast.29), kind=kLoop, calls=%fused_computation | loop fusion | flops 737280 | bytes 2162688 | tf_op jit(solution)/shard_map/add | solution.py:591

commit v6 on v5

--- a/solution.py
+++ b/solution.py
@@ -396,7 +396,7 @@
 
             @pl.when(r == last)
             def _():
-                lax.fori_loop(0, stacks, lambda k, c: share(k, c, pieces), 0)
+                lax.fori_loop(0, stacks, lambda k, c: share(lax.rem(m + k, stacks), c, pieces), 0)
 
         return carry
 

time: 50.3 us -> 50.2 us (level)
  no operation moved by 1% of the time
where the time goes in v6:
time: 50.2 us; the launch traced here: 50 us
  Pallas kernels  47.6 us (95%)
  between operations  1.31 us (3%)
  other arithmetic  1.09 us (2%)
    pallas_call x1, Pallas kernels, local(): pl.pallas_call(main_kernel, out_shape=[shape(DATES, 4 * ROWS, 128)] * 2 +...  39 us
    pallas_call x1, Pallas kernels, local(): pl.pallas_call(halo_kernel, out_shape=[shape(DATES, EXT, 8, 128), shape(D...  8.64 us
    add x1, other arithmetic, local(): out = linked_r * datum[:, None] + linked_i * turned[:, None]  1.09 us

profile of v6, /device:TPU:8, one launch (start us, length us, event | category | flops | bytes accessed | tf_op | source)
XLA Modules:
  0.0 50.0 jit_solution(11002050111242215140)
XLA Ops:
  1.3 8.6 %halo.1 = (f32[10,22,8,128]{3,2,1,0:T(8,128)S(1)}, f32[10,22,8,128]{3,2,1,0:T(8,128)S(1)}, f32[22,8,128]{2,1,0:T(8,128)S(1)}) custom-call(f32[10,3,4,8,128]{4,3,2,1,0:T(8,128)} %bitcast.33, f32[10,3,4,8,128]{4,3,2,1,0:T(8,128)} %bitcast.34, s32[3,4,8,128]{3,2,1,0:T(8,128)} %bitcast.35), custom_call_target="tpu_custom_call" | custom-call | tf_op jit(solution)/shard_map/halo/pallas_call | solution.py:536
  9.9 39.0 %power.1 = (f32[10,96,128]{2,1,0:T(8,128)S(1)}, f32[10,96,128]{2,1,0:T(8,128)S(1)}, f32[2,96,128]{2,1,0:T(8,128)S(1)}, f32[2,96,128]{2,1,0:T(8,128)S(1)}) custom-call(s32[1]{0:T(128)S(6)} %copy.6.iterations, s32[1]{0:T(128)S(6)} %copy.7.chosen, f32[10,22,8,128]{3,2,1,0:T(8,128)S(1)} %get-tuple-element.12.zr, f32[10,22,8,128]{3,2,1,0:T(8,128)S(1)} %get-tuple-element.13.zi, ...), custom_call_target="tpu_custom_call" | custom-call | tf_op jit(solution)/shard_map/power/pallas_call | solution.py:554
  49.0 1.1 %multiply_add_fusion = f32[2,10,24,512]{3,2,1,0:T(8,128)} fusion(f32[2,24,512]{2,1,0:T(8,128)S(1)} %bitcast.32, f32[10,24,512]{2,1,0:T(8,128)S(1)} %bitcast.30, f32[2,24,512]{2,1,0:T(8,128)S(1)} %bitcast.31, f32[10,24,512]{2,1,0:T(8,128)S(1)} %bitcast.29), kind=kLoop, calls=%fused_computation | loop fusion | flops 737280 | bytes 2162688 | tf_op jit(solution)/shard_map/add | solution.py:591
